TPU v7x, 256 devices: a whole 4x4x8 slice. The times are simulated.
256 devices in a mesh: rep: 4 (over x), ep: 64 (over y, z, core).
Axes of the slice: x: 4, y: 4, z: 8, core: 2. Of those that a mesh axis runs over, the one named last changes fastest.
Arguments:
- tokens: bfloat16 [32768, 2048], P(('rep', 'ep')), may hold values from -6 to 6
- expert_ids: int32 [32768, 2], P(('rep', 'ep')), may hold values from 0 to 63, all different within a row; in each aligned block of 128 rows (0 to 127, 128 to 255, ...) at most 5 rows name the same one
- route_weights: bfloat16 [32768, 2], P(('rep', 'ep')), may hold values from 0.099609375 to 1
- w_gate_up: bfloat16 [64, 2048, 1536], P('ep', 'rep'), may hold values from -0.125 to 0.125
- w_down: bfloat16 [64, 2048, 768], P('ep', 'rep'), may hold values from -0.21875 to 0.21875
- grad_out: bfloat16 [32768, 2048], P(('rep', 'ep')), may hold values from -1.5 to 1.5
Outputs:
- mixed: bfloat16 [32768, 2048], P(('rep', 'ep'))
- grad_tokens: bfloat16 [32768, 2048], P(('rep', 'ep'))
- grad_gate_up: bfloat16 [64, 2048, 1536], P('ep', 'rep')
- grad_down: bfloat16 [64, 2048, 768], P('ep', 'rep')
- route_grad: float32 [32768, 2], P(('rep', 'ep'))
Inputs may be any that keep to these rules, and one draw needn't show every extreme that they name: `expert_ids`: each token names 2 different experts. Among the rows of one device no expert is named more than 5 times, and in every draw some device names some expert exactly 5 times.
All inputs are finite; a program needn't handle non-finite values.
Results may differ from a plain program's by a relative error of at most 0.0095.
Values may be sent and summed in bfloat16 or wider, within the bound.
A program may use at most 128 MiB of HBM per device.

v0:
```python
import jax
import jax.numpy as jnp
from jax import lax
from jax.sharding import Mesh
from jax.sharding import PartitionSpec as P

EP = ("ep_0", "ep_1", "ep_2")
REP_EP = ("rep", "ep_0", "ep_1", "ep_2")


def split_up(x, dim, peers):
    lengths = x.shape
    pieces = x.reshape(*lengths[:dim], peers, lengths[dim] // peers, *lengths[dim + 1 :])
    return jnp.moveaxis(pieces, dim, 0)


def laid_out(pieces, dim):
    pieces = jnp.moveaxis(pieces, 0, dim)
    lengths = pieces.shape
    return pieces.reshape(*lengths[:dim], lengths[dim] * lengths[dim + 1], *lengths[dim + 2 :])


def turned_blocks(pieces, axes, turns):
    inside = pieces.shape[1:]
    out = pieces.reshape(*(lax.axis_size(a) for a in axes), *inside)
    for k in turns:
        out = lax.all_to_all(out, axes[k], k, k, tiled=True)
    return out.reshape(-1, *inside)


def exchange_by_chip(x, groups, turns, split_dim, concat_dim):
    peers = lax.axis_size(groups[0]) * lax.axis_size(groups[1])
    pieces = split_up(x, split_dim, peers)
    return laid_out(turned_blocks(pieces, groups, turns), concat_dim)


def exchange_in_groups(x, axis, split_dim, concat_dim, work, item_dim, out_dim):

    def moved(group):
        return lax.all_to_all(group, axis, split_axis=split_dim, concat_axis=concat_dim, tiled=True)

    items = jax.tree.leaves(x)[0].shape[item_dim]
    ends = [items * k // 2 for k in range(2 + 1)] if items % 2 == 0 else [0, items]
    groups = [
        jax.tree.map(lambda a: lax.slice_in_dim(a, low, high, axis=item_dim), x)
        for low, high in zip(ends, ends[1:])
    ]
    arrived = [moved(group) for group in groups]
    made = [work(group) for group in arrived]
    return jax.tree.map(lambda *parts: jnp.concatenate(parts, axis=out_dim), *made)


def swiglu_forward(slot_rows, weight_gu, weight_down):
    hidden_size = weight_down.shape[1]
    gate_up = jnp.dot(slot_rows, weight_gu, preferred_element_type=jnp.float32)
    gate_part = gate_up[:, :hidden_size]
    up_part = gate_up[:, hidden_size:]
    activated = (gate_part * jax.nn.sigmoid(gate_part) * up_part).astype(jnp.bfloat16)
    outputs = lax.dot_general(
        activated, weight_down, (((1,), (1,)), ((), ())), preferred_element_type=jnp.float32
    ).astype(jnp.bfloat16)
    return (gate_up, activated, outputs)


def swiglu_backward(cotangent, gate_up, weight_gu, weight_down):
    hidden_size = weight_down.shape[1]
    gate_part = gate_up[:, :hidden_size]
    up_part = gate_up[:, hidden_size:]
    grad_hidden = jnp.dot(cotangent, weight_down, preferred_element_type=jnp.float32)
    sigmoid_gate = jax.nn.sigmoid(gate_part)
    slope = sigmoid_gate * (1.0 + gate_part * (1.0 - sigmoid_gate))
    grad_gu = jnp.concatenate(
        [grad_hidden * up_part * slope, grad_hidden * gate_part * sigmoid_gate], axis=1
    ).astype(jnp.bfloat16)
    grad_rows = lax.dot_general(
        grad_gu, weight_gu, (((1,), (1,)), ((), ())), preferred_element_type=jnp.float32
    ).astype(jnp.bfloat16)
    return (grad_gu, grad_rows)


def per_device(tokens, expert_ids, route_weights, w_gate_up, w_down, grad_out):
    ep_size = lax.axis_size(EP)
    tok_rows = tokens.shape[0]
    top_count = expert_ids.shape[1]
    model_width = tokens.shape[1]
    hidden_size = w_down.shape[2]
    assign = tok_rows * top_count
    capacity = 5 * assign // (4 * ep_size)
    flat_ids = expert_ids.reshape(-1)
    one_hot = (flat_ids[:, None] == jnp.arange(ep_size, dtype=jnp.int32)[None, :]).astype(jnp.int32)
    rank = jnp.sum(jnp.cumsum(one_hot, axis=0) * one_hot, axis=1) - 1
    target = flat_ids * capacity + rank
    source = (
        jnp.full((ep_size * capacity,), assign, jnp.int32)
        .at[target]
        .set(jnp.arange(assign, dtype=jnp.int32))
    )
    token_of = source // top_count
    tokens_ext = jnp.concatenate([tokens, jnp.zeros((1, model_width), jnp.bfloat16)], axis=0)
    grad_ext = jnp.concatenate([grad_out, jnp.zeros((1, model_width), jnp.bfloat16)], axis=0)
    weight_ext = jnp.concatenate([route_weights.reshape(-1), jnp.zeros((1,), jnp.bfloat16)], axis=0)
    send_rows = tokens_ext[token_of].reshape(ep_size, capacity, model_width)
    send_grads = grad_ext[token_of].reshape(ep_size, capacity, model_width)
    send_weights = weight_ext[source].reshape(ep_size, capacity)
    full_gu, full_down = (
        lax.all_gather(w_gate_up[0], "rep", axis=0, tiled=True),
        lax.all_gather(w_down[0], "rep", axis=0, tiled=True),
    )

    def expert_forward(received):
        items = received.shape[1]
        gate_up, activated, outputs = swiglu_forward(
            received.reshape(-1, model_width), full_gu, full_down
        )
        out_back = exchange_by_chip(
            outputs.reshape(ep_size, items, model_width), (("ep_0", "ep_1"), "ep_2"), (1, 0), 0, 0
        )
        return (
            out_back,
            received,
            gate_up.reshape(ep_size, items, 2 * hidden_size),
            activated.reshape(ep_size, items, hidden_size),
        )

    out_back, kept_rows, kept_gu, kept_hidden = exchange_in_groups(
        send_rows, EP, 0, 0, expert_forward, 1, 1
    )
    send_cot = (
        send_weights.astype(jnp.float32)[:, :, None] * send_grads.astype(jnp.float32)
    ).astype(jnp.bfloat16)
    kept_cot = lax.all_to_all(send_cot, EP, split_axis=0, concat_axis=0, tiled=True)
    grad_gu, grad_rows = swiglu_backward(
        kept_cot.reshape(-1, model_width), kept_gu.reshape(-1, 2 * hidden_size), full_gu, full_down
    )
    rows_back = lax.all_to_all(
        grad_rows.reshape(ep_size, capacity, model_width),
        EP,
        split_axis=0,
        concat_axis=0,
        tiled=True,
    )
    slot_x = kept_rows.reshape(-1, model_width)
    slot_cot = kept_cot.reshape(-1, model_width)
    slot_hidden = kept_hidden.reshape(-1, hidden_size)
    column_block = slot_x
    grad_gate_up = lax.psum_scatter(
        lax.dot_general(
            column_block, grad_gu, (((0,), (0,)), ((), ())), preferred_element_type=jnp.float32
        ).astype(jnp.bfloat16),
        "rep",
        scatter_dimension=0,
        tiled=True,
    )
    column_block = slot_cot
    grad_down = lax.psum_scatter(
        lax.dot_general(
            column_block, slot_hidden, (((0,), (0,)), ((), ())), preferred_element_type=jnp.float32
        ).astype(jnp.bfloat16),
        "rep",
        scatter_dimension=0,
        tiled=True,
    )
    expert_out = (
        out_back.reshape(-1, model_width)[target]
        .reshape(tok_rows, top_count, model_width)
        .astype(jnp.float32)
    )
    mixed = jnp.sum(route_weights.astype(jnp.float32)[:, :, None] * expert_out, axis=1).astype(
        jnp.bfloat16
    )
    route_grad = jnp.sum(grad_out.astype(jnp.float32)[:, None, :] * expert_out, axis=2)
    grad_tokens = jnp.sum(
        rows_back.reshape(-1, model_width)[target]
        .reshape(tok_rows, top_count, model_width)
        .astype(jnp.float32),
        axis=1,
    ).astype(jnp.bfloat16)
    return (mixed, grad_tokens, grad_gate_up[None], grad_down[None], route_grad)


def solution(mesh):
    finer = Mesh(mesh.devices.reshape(mesh.shape["rep"], 4, 8, 2), ("rep", "ep_0", "ep_1", "ep_2"))
    placed = (
        P(REP_EP, None),
        P(REP_EP, None),
        P(REP_EP, None),
        P(EP, "rep", None),
        P(EP, "rep", None),
        P(REP_EP, None),
    )
    return jax.shard_map(
        per_device,
        mesh=finer,
        in_specs=placed,
        out_specs=(
            P(REP_EP, None),
            P(REP_EP, None),
            P(EP, "rep", None),
            P(EP, "rep", None),
            P(REP_EP, None),
        ),
        check_vma=False,
    )
```

profile of v0, /device:TPU:1, one launch (start us, length us, event | category | flops | bytes accessed | tf_op | source)
XLA Modules:
  0.0 283.4 jit_solution(8531572445340527498)
XLA Ops:
  7.2 0.0 all-gather.5.cloned.1.call-start
  7.2 0.7 all-gather.5.cloned.1.call-update
  7.9 0.8 copy.20
  8.7 0.1 eq.25
  8.8 0.1 eq.29
  9.0 0.7 broadcast_multiply_fusion
  9.7 0.1 copy.19
  9.8 0.1 mul.74
  9.9 0.6 reduce-window.6
  10.5 0.2 slice_reduce_fusion
  10.8 0.1 concatenate.13
  10.8 0.1 fusion.15
  11.0 1.4 scatter_custom_fusion
  12.4 2.4 gather_fusion
  14.9 1.6 reshape.111
  16.4 13.3 %all-to-all-start = ((bf16[64,5,2048]{2,1,0:T(8,128)(2,1)}), bf16[64,5,2048]{2,1,0:T(8,128)(2,1)S(1)}, u32[]{:S(2)}, u32[]{:S(2)}) async-start(bf16[64,5,2048]{2,1,0:T(8,128)(2,1)} %reshape.111), calls=%async_computation | async-start | bytes 4194304 | tf_op jit(solution)/shard_map/all_to_all | solution.py:40
  29.7 0.0 all-gather.7.cloned.1.call-start
  29.8 0.7 all-gather.7.cloned.1.call-update
  30.5 3.0 %gather_fusion.3 = bf16[320,2048]{1,0:T(8,128)(2,1)} fusion(bf16[129,2048]{1,0:T(8,128)(2,1)S(1)} %concatenate.15, s32[1024]{0:T(1024)S(1)} %get-tuple-element.18), kind=kCustom, calls=%fused_computation.3 | custom fusion | bytes 2622720 | tf_op jit(solution)/shard_map/gather | solution.py:103
  33.6 3.5 %reshape.120 = f32[64,5,2048]{2,1,0:T(8,128)} reshape(bf16[320,2048]{1,0:T(8,128)(2,1)} %gather_fusion.3) | data formatting | bytes 3932160 | tf_op jit(solution)/shard_map/convert_element_type | solution.py:129
  37.0 0.1 copy.26
  37.2 0.1 reshape.113
  37.3 2.5 gather_fusion.2
  39.8 0.1 reshape.119
  39.9 3.9 %multiply_convert_fusion = bf16[64,5,2048]{2,1,0:T(8,128)(2,1)} fusion(f32[64,5,2048]{2,1,0:T(8,128)} %reshape.120, f32[64,5]{1,0:T(8,128)S(1)} %reshape.119), kind=kLoop, calls=%fused_computation.11 | loop fusion | flops 1310720 | bytes 3933440 | tf_op jit(solution)/shard_map/convert_element_type | solution.py:130
  43.8 37.1 %all-to-all-done = bf16[64,5,2048]{2,1,0:T(8,128)(2,1)S(1)} async-done(((bf16[64,5,2048]{2,1,0:T(8,128)(2,1)}), bf16[64,5,2048]{2,1,0:T(8,128)(2,1)S(1)}, u32[]{:S(2)}, u32[]{:S(2)}) %all-to-all-start) | async-done | bytes 1310752 | tf_op jit(solution)/shard_map/all_to_all | solution.py:40
  80.9 6.0 %all-to-all-start.3 = ((bf16[64,5,2048]{2,1,0:T(8,128)(2,1)}), bf16[64,5,2048]{2,1,0:T(8,128)(2,1)}, u32[]{:S(2)}, u32[]{:S(2)}) async-start(bf16[64,5,2048]{2,1,0:T(8,128)(2,1)} %multiply_convert_fusion), calls=%async_computation.3 | async-start | bytes 4194304 | tf_op jit(solution)/shard_map/all_to_all | solution.py:131
  86.9 0.2 reduce-scatter.5.cloned.1.call-start
  87.2 0.6 reshape.112
  87.8 50.3 %all-to-all-done.3 = bf16[64,5,2048]{2,1,0:T(8,128)(2,1)} async-done(((bf16[64,5,2048]{2,1,0:T(8,128)(2,1)}), bf16[64,5,2048]{2,1,0:T(8,128)(2,1)}, u32[]{:S(2)}, u32[]{:S(2)}) %all-to-all-start.3) | async-done | bytes 1310752 | tf_op jit(solution)/shard_map/all_to_all | solution.py:131
  138.1 2.6 reshape.114
  140.6 0.0 all-gather.5.cloned.1.call-done
  140.7 6.3 %fusion.2 = f32[320,1536]{1,0:T(8,128)} fusion(bf16[320,2048]{1,0:T(8,128)(2,1)S(1)} %reshape.112, bf16[1,2048,1536]{2,1,0:T(8,128)(2,1)} %all-gather.5.cloned.1.call-done), kind=kOutput, calls=%fused_computation.9 | convolution fusion | flops 2013265920 | bytes 9568256 | tf_op jit(solution)/shard_map/dot_general | solution.py:55
  146.9 4.8 %multiply_convert_fusion.2 = (bf16[320,768]{1,0:T(8,128)(2,1)}, bf16[320,768]{1,0:T(8,128)(2,1)}, bf16[320,768]{1,0:T(8,128)(2,1)S(1)}) fusion(f32[320,1536]{1,0:T(8,128)} %fusion.2, bf16[320,2048]{1,0:T(8,128)(2,1)S(1)} %reshape.114, bf16[1,2048,768]{2,1,0:T(8,128)(2,1)} %all-gather.7.cloned.1.call-done), kind=kOutput, calls=%fused_computation.23 | convolution fusion | flops 1010565120 | bytes 7897088 | tf_op jit(solution)/shard_map/dot_general | solution.py:69
  151.7 3.5 %convolution_convert_fusion.1 = bf16[2048,768]{1,0:T(8,128)(2,1)} fusion(bf16[320,2048]{1,0:T(8,128)(2,1)S(1)} %reshape.114, bf16[320,768]{1,0:T(8,128)(2,1)S(1)} %get-tuple-element.14), kind=kOutput, calls=%fused_computation.12 | convolution fusion | flops 1008205824 | bytes 4947968 | tf_op jit(solution)/shard_map/dot_general | solution.py:156
  155.2 0.0 reduce-scatter.5.cloned.1.call-update
  155.2 0.0 reduce-scatter.3.cloned.1.call-start
  155.3 1.0 copy-done.4
  156.3 0.1 copy-done.6
  156.4 5.6 %convolution_convert_fusion = bf16[2048,1536]{1,0:T(8,128)(2,1)} fusion(bf16[320,2048]{1,0:T(8,128)(2,1)S(1)} %reshape.112, bf16[320,768]{1,0:T(8,128)(2,1)S(1)} %copy-done.6, bf16[320,768]{1,0:T(8,128)(2,1)S(1)} %copy-done.4), kind=kOutput, calls=%fused_computation.6 | convolution fusion | flops 2018377728 | bytes 8585216 | tf_op jit(solution)/shard_map/dot_general | solution.py:147
  162.0 0.0 reduce-scatter.3.cloned.1.call-update
  162.0 3.6 %fusion.11 = bf16[320,2048]{1,0:T(8,128)(2,1)S(1)} fusion(bf16[320,768]{1,0:T(8,128)(2,1)S(1)} %get-tuple-element.14, bf16[1,2048,768]{2,1,0:T(8,128)(2,1)} %all-gather.7.cloned.1.call-done), kind=kOutput, calls=%fused_computation.18 | convolution fusion | flops 1007288320 | bytes 4947968 | tf_op jit(solution)/shard_map/dot_general | solution.py:59
  165.6 0.6 reshape_reshape_reshape.6
  166.2 0.9 copy.23
  167.0 4.4 %all_to_all.25 = bf16[32,2,1,5,2048]{4,0,3,2,1:T(8,128)(2,1)S(1)} all-to-all(bf16[32,2,1,5,2048]{4,0,3,2,1:T(8,128)(2,1)S(1)} %copy.23), channel_id=1, replica_groups=mesh['rep'=4,'ep_0'=4,'ep_1'=8,'ep_2'=2] {'ep_2'}, dimensions={1} | all-to-all | bytes 2621440 | tf_op jit(solution)/shard_map/all_to_all | solution.py:27
  171.4 2.4 copy.24
  173.9 5.3 %all-to-all-start.2 = ((bf16[32,2,1,5,2048]{4,1,3,2,0:T(2,128)(2,1)}), bf16[32,2,1,5,2048]{4,1,3,2,0:T(2,128)(2,1)S(1)}, u32[]{:S(2)}, u32[]{:S(2)}) async-start(bf16[32,2,1,5,2048]{4,1,3,2,0:T(2,128)(2,1)} %copy.24), calls=%async_computation.2 | async-start | bytes 2621440 | tf_op jit(solution)/shard_map/all_to_all | solution.py:27
  179.1 5.3 %fusion.8 = bf16[320,2048]{1,0:T(8,128)(2,1)S(1)} fusion(bf16[1,2048,1536]{2,1,0:T(8,128)(2,1)} %all-gather.5.cloned.1.call-done, bf16[320,768]{1,0:T(8,128)(2,1)} %get-tuple-element.13, bf16[320,768]{1,0:T(8,128)(2,1)S(1)} %copy-done.5), kind=kOutput, calls=%fused_computation.17 | convolution fusion | flops 2015887360 | bytes 8585216 | tf_op jit(solution)/shard_map/dot_general | solution.py:75
  184.4 1.6 reshape.115
  186.0 24.6 %all-to-all-done.2 = bf16[32,2,1,5,2048]{4,1,3,2,0:T(2,128)(2,1)S(1)} async-done(((bf16[32,2,1,5,2048]{4,1,3,2,0:T(2,128)(2,1)}), bf16[32,2,1,5,2048]{4,1,3,2,0:T(2,128)(2,1)S(1)}, u32[]{:S(2)}, u32[]{:S(2)}) %all-to-all-start.2) | async-done | bytes 1310752 | tf_op jit(solution)/shard_map/all_to_all | solution.py:27
  210.6 8.8 %all-to-all-start.4 = ((bf16[64,5,2048]{2,1,0:T(8,128)(2,1)}), bf16[64,5,2048]{2,1,0:T(8,128)(2,1)S(1)}, u32[]{:S(2)}, u32[]{:S(2)}) async-start(bf16[64,5,2048]{2,1,0:T(8,128)(2,1)} %reshape.115), calls=%async_computation.4 | async-start | bytes 4194304 | tf_op jit(solution)/shard_map/all_to_all | solution.py:135
  219.4 2.2 convert_element_type.76
  221.5 0.1 copy.18
  221.6 2.0 copy.25
  223.6 2.6 reshape_reshape_reshape.7
  226.2 2.4 gather_fusion.1
  228.6 3.4 %reshape.118 = f32[128,2,2048]{2,1,0:T(2,128)} reshape(bf16[256,2048]{1,0:T(8,128)(2,1)} %gather_fusion.1) | data formatting | bytes 3145728 | tf_op jit(solution)/shard_map/convert_element_type | solution.py:166
  232.0 6.2 %multiply_reduce_fusion = (f32[128,2]{1,0:T(8,128)S(1)}, bf16[128,2048]{1,0:T(8,128)(2,1)}) fusion(f32[128,2,2048]{2,1,0:T(2,128)} %reshape.118, f32[128,2048]{1,0:T(8,128)S(1)} %copy-done, f32[128,2]{1,0:T(8,128)S(1)} %copy.18), kind=kLoop, calls=%fused_computation.19 | loop fusion | flops 1834752 | bytes 3672064 | tf_op jit(solution)/shard_map/reduce_sum | solution.py:171
  238.2 0.6 copy.27
  238.8 31.8 %all-to-all-done.4 = bf16[64,5,2048]{2,1,0:T(8,128)(2,1)S(1)} async-done(((bf16[64,5,2048]{2,1,0:T(8,128)(2,1)}), bf16[64,5,2048]{2,1,0:T(8,128)(2,1)S(1)}, u32[]{:S(2)}, u32[]{:S(2)}) %all-to-all-start.4) | async-done | bytes 1310752 | tf_op jit(solution)/shard_map/all_to_all | solution.py:135
  270.6 0.6 reshape.116
  271.1 1.4 gather_fusion.4
  272.5 0.7 reshape.117
  273.2 3.6 %reduce_sum.41 = bf16[128,2048]{1,0:T(8,128)(2,1)} reduce(bf16[128,2,2048]{2,1,0:T(2,128)(2,1)S(1)} %reshape.117, bf16[]{:T(256)} %constant.13.clone.1), dimensions={1}, to_apply=%region_5.6 | reduce | flops 262144 | bytes 1572866 | tf_op jit(solution)/shard_map/reduce_sum | solution.py:172
  (26 shorter events, 0.2 us)
Async XLA Ops:
  7.2 3.6 %copy-start.2 = (bf16[128,2048]{1,0:T(8,128)(2,1)S(1)}, bf16[128,2048]{1,0:T(8,128)(2,1)}, u32[]{:S(2)}) copy-start(bf16[128,2048]{1,0:T(8,128)(2,1)} %param.6) | copy-start | bytes 1572868
  7.2 133.5 %all-gather.5.cloned.1.call-start = ((), (), s32[]{:S(2)}) async-start(), calls=%async_computation.9 | async-start | bytes 7864320 | tf_op jit(solution)/shard_map/all_gather | solution.py:106
  16.4 14.0 %copy-start.1 = (bf16[128,2048]{1,0:T(8,128)(2,1)S(1)}, bf16[128,2048]{1,0:T(8,128)(2,1)}, u32[]{:S(2)}) copy-start(bf16[128,2048]{1,0:T(8,128)(2,1)} %param.11) | copy-start | bytes 1572868
  16.4 64.5 %all-to-all-start = ((bf16[64,5,2048]{2,1,0:T(8,128)(2,1)}), bf16[64,5,2048]{2,1,0:T(8,128)(2,1)S(1)}, u32[]{:S(2)}, u32[]{:S(2)}) async-start(bf16[64,5,2048]{2,1,0:T(8,128)(2,1)} %reshape.111), calls=%async_computation | async-start | bytes 4194304 | tf_op jit(solution)/shard_map/all_to_all | solution.py:40
  29.7 117.2 %all-gather.7.cloned.1.call-start = ((), (), s32[]{:S(2)}) async-start(), calls=%async_computation.10 | async-start | bytes 3932160 | tf_op jit(solution)/shard_map/all_gather | solution.py:107
  33.5 3.5 %copy-start.3 = (bf16[128,2]{0,1:T(2,128)(2,1)S(1)}, bf16[128,2]{0,1:T(2,128)(2,1)}, u32[]{:S(2)}) copy-start(bf16[128,2]{0,1:T(2,128)(2,1)} %param.8) | copy-start | bytes 1540
  80.9 57.1 %all-to-all-start.3 = ((bf16[64,5,2048]{2,1,0:T(8,128)(2,1)}), bf16[64,5,2048]{2,1,0:T(8,128)(2,1)}, u32[]{:S(2)}, u32[]{:S(2)}) async-start(bf16[64,5,2048]{2,1,0:T(8,128)(2,1)} %multiply_convert_fusion), calls=%async_computation.3 | async-start | bytes 4194304 | tf_op jit(solution)/shard_map/all_to_all | solution.py:131
  86.9 189.9 %reduce-scatter.5.cloned.1.call-start = ((), (), s32[]{:S(2)}) async-start(), calls=%async_computation.8 | async-start | bytes 3932160 | tf_op jit(solution)/shard_map/reduce_scatter | solution.py:155
  155.2 1.0 copy-start.4
  155.2 1.2 copy-start.6
  155.2 121.6 %reduce-scatter.3.cloned.1.call-start = ((), (), s32[]{:S(2)}) async-start(), calls=%async_computation.7 | async-start | bytes 7864320 | tf_op jit(solution)/shard_map/reduce_scatter | solution.py:146
  173.9 5.3 %copy-start.5 = (bf16[320,768]{1,0:T(8,128)(2,1)S(1)}, bf16[320,768]{1,0:T(8,128)(2,1)}, u32[]{:S(2)}) copy-start(bf16[320,768]{1,0:T(8,128)(2,1)} %get-tuple-element.12) | copy-start | bytes 1474564
  173.9 36.7 %all-to-all-start.2 = ((bf16[32,2,1,5,2048]{4,1,3,2,0:T(2,128)(2,1)}), bf16[32,2,1,5,2048]{4,1,3,2,0:T(2,128)(2,1)S(1)}, u32[]{:S(2)}, u32[]{:S(2)}) async-start(bf16[32,2,1,5,2048]{4,1,3,2,0:T(2,128)(2,1)} %copy.24), calls=%async_computation.2 | async-start | bytes 2621440 | tf_op jit(solution)/shard_map/all_to_all | solution.py:27
  210.6 60.0 %all-to-all-start.4 = ((bf16[64,5,2048]{2,1,0:T(8,128)(2,1)}), bf16[64,5,2048]{2,1,0:T(8,128)(2,1)S(1)}, u32[]{:S(2)}, u32[]{:S(2)}) async-start(bf16[64,5,2048]{2,1,0:T(8,128)(2,1)} %reshape.115), calls=%async_computation.4 | async-start | bytes 4194304 | tf_op jit(solution)/shard_map/all_to_all | solution.py:135
  228.6 3.4 %copy-start = (f32[128,2048]{1,0:T(8,128)S(1)}, f32[128,2048]{1,0:T(8,128)}, u32[]{:S(2)}) copy-start(f32[128,2048]{1,0:T(8,128)} %convert_element_type.76) | copy-start | bytes 3145732
Sparse Core Ops, SparseCore 0:
  9.8 71.7 all-gather.4
  83.4 42.6 all-gather.6
  155.4 37.2 reduce-scatter.4
  195.6 66.2 reduce-scatter.2
where the time goes:
time: 284 us; the launch traced here: 283 us
  waiting for transfers between devices  145 us (51%)
  local copies, waits for them, and re-layouts  39.8 us (14%)
  starting transfers between devices  33.7 us (12%)
  matrix products  29 us (10%)
  other arithmetic  17.3 us (6%)
  between operations  14 us (5%)
  blocking collectives  4.42 us (2%)
    all_to_all x1, waiting for transfers between devices, per_device(): lax.all_to_all(send_cot, EP, split_axis=0, concat_axis=0, tiled=True)  50.3 us
    all_to_all x1, waiting for transfers between devices, moved(): lax.all_to_all(group, axis, split_axis=split_dim, concat_axis=concat_dim,...  37.1 us
    all_to_all x1, waiting for transfers between devices, per_device(): lax.all_to_all(grad_rows.reshape(ep_size, capacity, model_width), EP, spl...  31.8 us
    all_to_all x1, waiting for transfers between devices, turned_blocks(): out = lax.all_to_all(out, axes[k], k, k, tiled=True)  24.6 us
    all_to_all x1, starting transfers between devices, moved(): lax.all_to_all(group, axis, split_axis=split_dim, concat_axis=concat_dim,...  13.3 us
    all_to_all x1, starting transfers between devices, per_device(): lax.all_to_all(grad_rows.reshape(ep_size, capacity, model_width), EP, spl...  8.79 us
    dot_general x1, matrix products, swiglu_forward(): gate_up = jnp.dot(slot_rows, weight_gu, preferred_element_type=jnp.float32)  6.27 us
    reduce_sum x1, other arithmetic, per_device(): jnp.sum(grad_out.astype(jnp.float32)[:, None, :] * expert_out, axis=2)  6.17 us
  transfers between devices with their start and end apart: 8, of which 4 were waited for; matrix products, arithmetic and copies ran while one was open for 27% of the time, Pallas kernels for 0%

commit v1 on v0

v1 whole, which is shorter than its diff:
```python
import functools

import jax
import jax.numpy as jnp
from jax import lax
from jax.experimental import pallas as pl
from jax.experimental.pallas import tpu as pltpu
from jax.sharding import PartitionSpec as P

MESH = pl.DeviceIdType.MESH
F32 = jnp.float32
BF16 = jnp.bfloat16
LANES = 128


def layer_kernel(
    sizes,
    source_ref,
    slot_weight_ref,
    target_ref,
    pair_weight_ref,
    tokens_ref,
    grad_ref,
    wg_hbm,
    wd_hbm,
    mixed_ref,
    gtok_ref,
    ggu_ref,
    gdn_ref,
    rg_ref,
    wg,
    wd,
    own_g,
    own_d,
    part_g,
    part_d,
    rin_g,
    rin_d,
    din_g,
    din_d,
    send_x,
    recv_x,
    send_c,
    recv_c,
    send_o,
    recv_o,
    send_r,
    recv_r,
    x2,
    c2,
    scr,
    acc,
    gh,
    hid,
    ggu,
    tok_t,
    grd_t,
    rg_a,
    rg_b,
    local_sem,
    ag_send,
    ag_recv,
    rl_send,
    rl_recv,
    ro_send,
    ro_recv,
    rs_send,
    rs_recv,
    a2a_send,
    a2a_recv,
):
    n_rep, n_ep, cap, tok, width, hidden = sizes
    quarter = width // n_rep
    half = quarter // 2
    tiles = width // LANES
    per_q = quarter // LANES
    slots = n_ep * cap
    x = lax.axis_index("rep")
    e = lax.axis_index("ep")
    right = lax.rem(x + 1, n_rep)
    left = lax.rem(x + n_rep - 1, n_rep)
    quarters = (x, left, right, lax.rem(x + 2, n_rep))

    barrier = pltpu.get_barrier_semaphore()
    for side in (left, right):
        pl.semaphore_signal(barrier, inc=1, device_id=(side, e), device_id_type=MESH)

    @pl.loop(1, n_ep)
    def _(i):
        pl.semaphore_signal(
            barrier, inc=1, device_id=(x, lax.rem(e + i, n_ep)), device_id_type=MESH
        )

    local = [
        pltpu.make_async_copy(wg_hbm, wg.at[0], local_sem.at[0]),
        pltpu.make_async_copy(wd_hbm, wd.at[0], local_sem.at[1]),
    ]
    for copy in local:
        copy.start()

    hbm = (wg_hbm, wd_hbm)
    full = (wg, wd)
    part = (part_g, part_d)
    rin = (rin_g, rin_d)
    din = (din_g, din_d)
    own = (own_g, own_d)
    halves = (pl.ds(0, half), pl.ds(half, half))
    sides = (right, left)

    def gather_copy(k, d, h):
        return pltpu.make_async_remote_copy(
            src_ref=hbm[k].at[halves[h], :],
            dst_ref=full[k].at[1 + d, halves[h], :],
            send_sem=ag_send.at[k, d, h],
            recv_sem=ag_recv.at[k, d, h],
            device_id=(sides[d], e),
            device_id_type=MESH,
        )

    def relay_copy(k, d):
        return pltpu.make_async_remote_copy(
            src_ref=full[k].at[1 + d, halves[d], :],
            dst_ref=full[k].at[3, halves[d], :],
            send_sem=rl_send.at[k, d],
            recv_sem=rl_recv.at[k, d],
            device_id=(sides[d], e),
            device_id_type=MESH,
        )

    def far_copy(k, d):
        return pltpu.make_async_remote_copy(
            src_ref=part[k].at[2, halves[d], :],
            dst_ref=rin[k].at[d],
            send_sem=ro_send.at[k, d],
            recv_sem=ro_recv.at[k, d],
            device_id=(sides[d], e),
            device_id_type=MESH,
        )

    def near_copy(k, d, h):
        return pltpu.make_async_remote_copy(
            src_ref=part[k].at[1 - d, halves[h], :],
            dst_ref=din[k].at[d, halves[h], :],
            send_sem=rs_send.at[k, d, h],
            recv_sem=rs_recv.at[k, d, h],
            device_id=(sides[d], e),
            device_id_type=MESH,
        )

    def send_all(send, recv, n):
        @pl.loop(1, n_ep)
        def _(i):
            peer = lax.rem(e + i, n_ep)
            pltpu.make_async_remote_copy(
                src_ref=send.at[pl.ds(peer * cap, cap)],
                dst_ref=recv.at[pl.ds(e * cap, cap)],
                send_sem=a2a_send.at[n],
                recv_sem=a2a_recv.at[n],
                device_id=(x, peer),
                device_id_type=MESH,
            ).start()

        mine = pl.ds(e * cap, cap)
        recv[mine] = send[mine]

    def wait_all(buf, sem):
        rest = buf.at[pl.ds(0, (n_ep - 1) * cap)]
        pltpu.make_async_copy(rest, rest, sem).wait()

    def tiled(src, dst):
        for s in range(n_rep):
            for j in range(per_q):
                col = pl.multiple_of(quarters[s] * quarter + j * LANES, LANES)
                scr[pl.ds(s * per_q + j, tok, stride=tiles), :] = src[:, pl.ds(col, LANES)].astype(F32)

        @pl.loop(0, tok // 8)
        def _(i):
            rows = pl.ds(pl.multiple_of(i * 8 * tiles, 16), 8 * tiles)
            dst[pl.ds(i * 8, 8)] = scr[rows, :].astype(BF16).reshape(8, tiles, LANES)

        dst[tok] = jnp.zeros((tiles, LANES), BF16)

    def row(r):
        return pl.ds(pl.multiple_of(r * tiles, 16), tiles)

    tiled(tokens_ref, tok_t)

    @pl.loop(0, slots // 8)
    def _(i):
        for j in range(8):
            s = i * 8 + j
            send_x[s] = tok_t[source_ref[s]]

    pl.semaphore_wait(barrier, n_ep + 1)
    for k in range(2):
        for h in range(2):
            for d in range(2):
                gather_copy(k, d, h ^ d).start()
    send_all(send_x, recv_x, 0)

    tiled(grad_ref, grd_t)

    @pl.loop(0, slots // 8)
    def _(i):
        for j in range(8):
            s = i * 8 + j
            rows = grd_t[source_ref[s]].astype(F32) * slot_weight_ref[s]
            send_c[s] = rows.astype(BF16)

    send_all(send_c, recv_c, 1)

    def spread(recv, dst):
        @pl.loop(0, slots // 8)
        def _(i):
            rows = pl.ds(pl.multiple_of(i * 8 * tiles, 16), 8 * tiles)
            scr[rows, :] = recv[pl.ds(i * 8, 8)].astype(F32).reshape(8 * tiles, LANES)

        for s in range(n_rep):
            for j in range(per_q):
                dst[s, :, j * LANES : (j + 1) * LANES] = scr[
                    pl.ds(s * per_q + j, slots, stride=tiles), :
                ].astype(BF16)

    def product(s, lhs, rhs, out, columns, step, first):
        @pl.loop(0, columns // step)
        def _(n):
            cols = pl.ds(pl.multiple_of(n * step, LANES), step)
            y = jnp.dot(lhs[s], rhs[s, :, cols], preferred_element_type=F32)
            if first:
                out[:, cols] = y
            else:
                out[:, cols] = out[:, cols] + y

    def returned(lhs, rhs, send, n_blocks):
        for s in range(n_rep):
            for j in range(per_q):
                scr[pl.ds(s * per_q + j, slots, stride=tiles), :] = lax.dot_general(
                    lhs[...],
                    rhs[s, j * LANES : (j + 1) * LANES, :],
                    (((1,), (1,)), ((), ())),
                    preferred_element_type=F32,
                )

        @pl.loop(0, slots // 8)
        def _(i):
            rows = pl.ds(pl.multiple_of(i * 8 * tiles, 16), 8 * tiles)
            send[pl.ds(i * 8, 8)] = scr[rows, :].astype(BF16).reshape(8, tiles, LANES)

    def outer(lhs, rhs, s, h, k, columns, step):
        block = lhs[s, :, h * half : (h + 1) * half]

        @pl.loop(0, columns // step)
        def _(n):
            cols = pl.ds(pl.multiple_of(n * step, LANES), step)
            y = lax.dot_general(
                block, rhs[:, cols], (((0,), (0,)), ((), ())), preferred_element_type=F32
            )
            if s == 0:
                own[k][halves[h], cols] = y
            else:
                part[k][s - 1, halves[h], cols] = y.astype(BF16)

    def partial_grads(lhs, rhs, k, columns, step):
        for d in range(2):
            outer(lhs, rhs, 3, d, k, columns, step)
            far_copy(k, d).start()
        for d in range(2):
            outer(lhs, rhs, 2 - d, 1 - d, k, columns, step)
            near_copy(k, d, 1 - d).start()
        for d in range(2):
            outer(lhs, rhs, 2 - d, d, k, columns, step)

    def pass_on(k):
        for d in range(2):
            far_copy(k, d).wait_recv()

            @pl.loop(0, half // 16)
            def _(i):
                here = pl.ds(pl.multiple_of(i * 16, 16), 16)
                there = pl.ds(pl.multiple_of(d * half + i * 16, 16), 16)
                total = part[k][1 - d, there, :].astype(F32) + rin[k][d, here, :].astype(F32)
                part[k][1 - d, there, :] = total.astype(BF16)

            near_copy(k, d, d).start()

    def finish(k, out):
        for h in range(2):
            for d in range(2):
                near_copy(k, d, h).wait_recv()

            @pl.loop(0, half // 16)
            def _(i):
                rows = pl.ds(pl.multiple_of(h * half + i * 16, 16), 16)
                total = own[k][rows, :] + din[k][0, rows, :].astype(F32) + din[k][1, rows, :].astype(F32)
                out[rows, :] = total.astype(BF16)

    wait_all(recv_x, a2a_recv.at[0])
    spread(recv_x, x2)
    local[0].wait()
    product(0, x2, wg, acc, 2 * hidden, 256, True)
    for d in range(2):
        gather_copy(0, d, d).wait_recv()
        relay_copy(0, d).start()
    for d in range(2):
        gather_copy(0, d, 1 - d).wait_recv()
        product(1 + d, x2, wg, acc, 2 * hidden, 256, False)
    for d in range(2):
        gather_copy(1, d, d).wait_recv()
        relay_copy(1, d).start()
    wait_all(recv_c, a2a_recv.at[1])
    spread(recv_c, c2)
    local[1].wait()
    product(0, c2, wd, gh, hidden, 256, True)
    for d in range(2):
        gather_copy(1, d, 1 - d).wait_recv()
        product(1 + d, c2, wd, gh, hidden, 256, False)
    for d in range(2):
        relay_copy(0, d).wait_recv()
    product(3, x2, wg, acc, 2 * hidden, 256, False)

    @pl.loop(0, slots // 16)
    def _(i):
        rows = pl.ds(pl.multiple_of(i * 16, 16), 16)
        gate = acc[rows, :hidden]
        up = acc[rows, hidden:]
        hid[rows, :] = (gate * jax.nn.sigmoid(gate) * up).astype(BF16)

    partial_grads(c2, hid, 1, hidden, 256)
    for d in range(2):
        relay_copy(1, d).wait_recv()
    product(3, c2, wd, gh, hidden, 256, False)

    @pl.loop(0, slots // 16)
    def _(i):
        rows = pl.ds(pl.multiple_of(i * 16, 16), 16)
        gate = acc[rows, :hidden]
        up = acc[rows, hidden:]
        grad = gh[rows, :]
        s = jax.nn.sigmoid(gate)
        ggu[rows, :hidden] = (grad * up * (s * (1.0 + gate * (1.0 - s)))).astype(BF16)
        ggu[rows, hidden:] = (grad * gate * s).astype(BF16)

    returned(hid, wd, send_o, 0)
    send_all(send_o, recv_o, 2)
    pass_on(1)
    partial_grads(x2, ggu, 0, 2 * hidden, 256)
    returned(ggu, wg, send_r, 0)
    send_all(send_r, recv_r, 3)
    for h in range(2):
        outer(c2, hid, 0, h, 1, hidden, 256)
    for h in range(2):
        outer(x2, ggu, 0, h, 0, 2 * hidden, 256)
    pass_on(0)
    finish(1, gdn_ref)

    def untiled(out):
        for s in range(n_rep):
            for j in range(per_q):
                col = pl.multiple_of(quarters[s] * quarter + j * LANES, LANES)
                out[:, pl.ds(col, LANES)] = scr[pl.ds(s * per_q + j, tok, stride=tiles), :].astype(BF16)

    wait_all(recv_o, a2a_recv.at[2])

    @pl.loop(0, tok // 4)
    def _(i):
        for j in range(4):
            t = i * 4 + j
            first = recv_o[target_ref[2 * t]].astype(F32)
            second = recv_o[target_ref[2 * t + 1]].astype(F32)
            grad = grd_t[t].astype(F32)
            scr[row(t), :] = pair_weight_ref[2 * t] * first + pair_weight_ref[2 * t + 1] * second
            rg_a[pl.ds(t, 1), :] = jnp.sum(grad * first, axis=0, keepdims=True)
            rg_b[pl.ds(t, 1), :] = jnp.sum(grad * second, axis=0, keepdims=True)

    untiled(mixed_ref)
    rg_ref[:, 0:1] = jnp.sum(rg_a[...], axis=1, keepdims=True)
    rg_ref[:, 1:2] = jnp.sum(rg_b[...], axis=1, keepdims=True)

    wait_all(recv_r, a2a_recv.at[3])

    @pl.loop(0, tok // 4)
    def _(i):
        for j in range(4):
            t = i * 4 + j
            first = recv_r[target_ref[2 * t]].astype(F32)
            second = recv_r[target_ref[2 * t + 1]].astype(F32)
            scr[row(t), :] = first + second

    untiled(gtok_ref)
    finish(0, ggu_ref)

    for n, buf in enumerate((send_x, send_c, send_o, send_r)):
        wait_all(buf, a2a_send.at[n])
    for k in range(2):
        for d in range(2):
            relay_copy(k, d).wait_send()
            far_copy(k, d).wait_send()
            for h in range(2):
                gather_copy(k, d, h).wait_send()
                near_copy(k, d, h).wait_send()


def routing(expert_ids, route_weights, n_ep, cap):
    assign = expert_ids.size
    flat = expert_ids.reshape(-1)
    order = jnp.arange(assign, dtype=jnp.int32)
    earlier = (flat[:, None] == flat[None, :]) & (order[None, :] < order[:, None])
    target = flat * cap + jnp.sum(earlier.astype(jnp.int32), axis=1)
    slot = jnp.arange(n_ep * cap, dtype=jnp.int32)
    match = slot[:, None] == target[None, :]
    top = expert_ids.shape[1]
    found = jnp.where(match, (order // top)[None, :] - expert_ids.shape[0], 0)
    source = jnp.sum(found, axis=1) + expert_ids.shape[0]
    weights = route_weights.reshape(-1).astype(F32)
    slot_weight = jnp.sum(jnp.where(match, weights[None, :], 0.0), axis=1)
    return source, slot_weight, target, weights


def per_device(n_rep, n_ep, tokens, expert_ids, route_weights, w_gate_up, w_down, grad_out):
    tok, width = tokens.shape
    top = expert_ids.shape[1]
    hidden = w_down.shape[2]
    cap = 5 * tok * top // (4 * n_ep)
    slots = n_ep * cap
    quarter = width // n_rep
    half = quarter // 2
    tiles = width // LANES
    source, slot_weight, target, weights = routing(expert_ids, route_weights, n_ep, cap)
    smem = pl.BlockSpec(memory_space=pltpu.SMEM)
    vmem = pl.BlockSpec(memory_space=pltpu.VMEM)
    anywhere = pl.BlockSpec(memory_space=pl.ANY)
    V = pltpu.VMEM
    rows = V((slots, tiles, LANES), BF16)
    dma = pltpu.SemaphoreType.DMA
    mixed, gtok, ggu, gdn, rg = pl.pallas_call(
        functools.partial(layer_kernel, (n_rep, n_ep, cap, tok, width, hidden)),
        out_shape=(
            jax.ShapeDtypeStruct((tok, width), BF16),
            jax.ShapeDtypeStruct((tok, width), BF16),
            jax.ShapeDtypeStruct((quarter, 2 * hidden), BF16),
            jax.ShapeDtypeStruct((quarter, hidden), BF16),
            jax.ShapeDtypeStruct((tok, top), F32),
        ),
        in_specs=[smem] * 4 + [vmem] * 2 + [anywhere] * 2,
        out_specs=[vmem] * 5,
        scratch_shapes=[
            V((n_rep, quarter, 2 * hidden), BF16),
            V((n_rep, quarter, hidden), BF16),
            V((quarter, 2 * hidden), F32),
            V((quarter, hidden), F32),
            V((n_rep - 1, quarter, 2 * hidden), BF16),
            V((n_rep - 1, quarter, hidden), BF16),
            V((2, half, 2 * hidden), BF16),
            V((2, half, hidden), BF16),
            V((2, quarter, 2 * hidden), BF16),
            V((2, quarter, hidden), BF16),
        ]
        + [rows] * 8
        + [
            V((n_rep, slots, quarter), BF16),
            V((n_rep, slots, quarter), BF16),
            V((slots * tiles, LANES), F32),
            V((slots, 2 * hidden), F32),
            V((slots, hidden), F32),
            V((slots, hidden), BF16),
            V((slots, 2 * hidden), BF16),
            V((tok + 1, tiles, LANES), BF16),
            V((tok + 1, tiles, LANES), BF16),
            V((tok, LANES), F32),
            V((tok, LANES), F32),
            dma((2,)),
            dma((2, 2, 2)),
            dma((2, 2, 2)),
            dma((2, 2)),
            dma((2, 2)),
            dma((2, 2)),
            dma((2, 2)),
            dma((2, 2, 2)),
            dma((2, 2, 2)),
            dma((4,)),
            dma((4,)),
        ],
        compiler_params=pltpu.CompilerParams(
            collective_id=0, has_side_effects=True, vmem_limit_bytes=67043328
        ),
    )(source, slot_weight, target, weights, tokens, grad_out, w_gate_up[0], w_down[0])
    return mixed, gtok, ggu[None], gdn[None], rg


def solution(mesh):
    both = ("rep", "ep")
    split = P(both, None)
    weights = P("ep", "rep", None)
    return jax.shard_map(
        functools.partial(per_device, mesh.shape["rep"], mesh.shape["ep"]),
        mesh=mesh,
        in_specs=(split, split, split, weights, weights, split),
        out_specs=(split, split, weights, weights, split),
        check_vma=False,
    )
```

time: 284 us -> 184 us (0.65)
  Pallas kernels: 0 us -> 171 us
  waiting for transfers between devices: 145 us -> 0 us
  starting transfers between devices: 33.7 us -> 0 us
  local copies, waits for them, and re-layouts: 39.8 us -> 10.3 us
  matrix products: 29 us -> 0 us
  other arithmetic: 17.3 us -> 1.65 us
  between operations: 14 us -> 0.69 us
  blocking collectives: 4.42 us -> 0 us
    pallas_call x0 -> x1, Pallas kernels: none -> 171 us  [per_device(): pl.pallas_call(functools.partial(layer_kernel, (n_rep, n_ep, cap, tok, wi...]
    all_to_all x4 -> x0, waiting for transfers between devices: 144 us -> none  [the longest x1 50.3 us: per_device(): lax.all_to_all(send_cot, EP, split_axis=0, concat_axis=0, tiled=True)]
    all_to_all x4 -> x0, starting transfers between devices: 33.3 us -> none  [the longest x1 13.3 us: moved(): lax.all_to_all(group, axis, split_axis=split_dim, concat_axis=concat_dim,...]
    dot_general x6 -> x0, matrix products: 29 us -> none  [the longest x1 6.27 us: swiglu_forward(): gate_up = jnp.dot(slot_rows, weight_gu, preferred_element_type=jnp.float32)]
    gather x5 -> x0, local copies, waits for them, and re-layouts: 11.6 us -> none  [the longest x1 3.02 us: per_device(): send_grads = grad_ext[token_of].reshape(ep_size, capacity, model_width)]
    reduce_sum x3, other arithmetic: 9.89 us -> 1.06 us  [the longest x1 0.73 us: routing(): slot_weight = jnp.sum(jnp.where(match, weights[None, :], 0.0), axis=1)]
    reshape x7 -> x1, local copies, waits for them, and re-layouts: 7.75 us -> 0.14 us  [routing(): flat = expert_ids.reshape(-1)]
    unnamed x17 -> x14, local copies, waits for them, and re-layouts: 2.68 us -> 9.26 us
  transfers between devices with their start and end apart: 8 -> 0, of which waited for: 4 -> 0; matrix products, arithmetic and copies ran while one was open for 27% -> 0% of each run, Pallas kernels for 0% -> 0%
where the time goes in v1:
time: 184 us; the launch traced here: 183 us
  Pallas kernels  171 us (93%)
  local copies, waits for them, and re-layouts  10.3 us (6%)
    pallas_call x1, Pallas kernels, per_device(): pl.pallas_call(functools.partial(layer_kernel, (n_rep, n_ep, cap, tok, wi...  171 us
    unnamed x14, local copies, waits for them, and re-layouts  9.26 us

profile of v1, /device:TPU:1, one launch (start us, length us, event | category | flops | bytes accessed | tf_op | source)
XLA Modules:
  0.0 183.3 jit_solution(8565487615301423792)
XLA Ops:
  0.6 0.8 copy.15
  1.4 0.1 reshape.46
  1.6 0.2 convert_reduce_fusion
  1.8 0.0 copy-start.2
  1.8 0.1 select_reduce_fusion.1
  1.9 0.6 broadcast_add_fusion.source_ref
  2.5 0.8 copy.16
  3.3 0.1 reshape.47.pair_weight_ref
  3.4 0.0 copy-done.2
  3.4 0.0 copy-start.3
  3.4 0.6 copy-done.3
  4.0 0.7 select_reduce_fusion.slot_weight_ref
  4.7 170.6 %shard_map.101 = (bf16[128,2048]{1,0:T(8,128)(2,1)}, bf16[128,2048]{1,0:T(8,128)(2,1)}, bf16[512,1536]{1,0:T(8,128)(2,1)}, bf16[512,768]{1,0:T(8,128)(2,1)}, f32[128,2]{1,0:T(8,128)}) custom-call(s32[320]{0:T(512)} %broadcast_add_fusion.source_ref, f32[320]{0:T(512)} %select_reduce_fusion.slot_weight_ref, s32[256]{0:T(256)} %copy-done.2, f32[256]{0:T(256)} %copy-done.3, ...), custom_call_target="tpu_custom_call" | custom-call | tf_op jit(solution)/shard_map/pallas_call | solution.py:435
  175.3 0.0 copy-start
  175.4 1.6 copy.17
  176.9 1.9 %copy.22 = bf16[128,2048]{1,0:T(8,128)(2,1)} copy(bf16[128,2048]{1,0:T(8,128)(2,1)} %get-tuple-element.37) | data formatting | bytes 1048576
  178.8 1.9 %copy.23 = bf16[128,2048]{1,0:T(8,128)(2,1)} copy(bf16[128,2048]{1,0:T(8,128)(2,1)} %get-tuple-element.38) | data formatting | bytes 1048576
  180.7 0.0 copy-done
  180.7 0.0 copy-start.1
  180.7 1.1 copy.24
  181.9 0.5 copy-done.1
  182.4 0.9 copy.25
  (1 shorter events, 0.0 us)
Async XLA Ops:
  1.8 1.7 copy-start.2
  3.4 0.6 copy-start.3
  175.3 5.4 %copy-start = (bf16[512,1536]{1,0:T(8,128)(2,1)S(1)}, bf16[512,1536]{1,0:T(8,128)(2,1)}, u32[]{:S(2)}) copy-start(bf16[512,1536]{1,0:T(8,128)(2,1)} %get-tuple-element.12) | copy-start | bytes 4718596
  180.7 1.7 copy-start.1

commit v2 on v1

--- a/solution.py
+++ b/solution.py
@@ -15,10 +15,8 @@
 
 def layer_kernel(
     sizes,
-    source_ref,
-    slot_weight_ref,
-    target_ref,
-    pair_weight_ref,
+    ids_ref,
+    pair_ref,
     tokens_ref,
     grad_ref,
     wg_hbm,
@@ -57,6 +55,10 @@
     grd_t,
     rg_a,
     rg_b,
+    index_v,
+    weight_v,
+    index_s,
+    weight_s,
     local_sem,
     ag_send,
     ag_recv,
@@ -183,13 +185,22 @@
     def row(r):
         return pl.ds(pl.multiple_of(r * tiles, 16), tiles)
 
+    tables = [
+        pltpu.make_async_copy(index_v, index_s, local_sem.at[2]),
+        pltpu.make_async_copy(weight_v, weight_s, local_sem.at[3]),
+    ]
+    routing(ids_ref, pair_ref, index_v, weight_v, cap)
+    for copy in tables:
+        copy.start()
     tiled(tokens_ref, tok_t)
+    for copy in tables:
+        copy.wait()
 
     @pl.loop(0, slots // 8)
     def _(i):
         for j in range(8):
             s = i * 8 + j
-            send_x[s] = tok_t[source_ref[s]]
+            send_x[s] = tok_t[index_s[0, s]]
 
     pl.semaphore_wait(barrier, n_ep + 1)
     for k in range(2):
@@ -204,7 +215,7 @@
     def _(i):
         for j in range(8):
             s = i * 8 + j
-            rows = grd_t[source_ref[s]].astype(F32) * slot_weight_ref[s]
+            rows = grd_t[index_s[0, s]].astype(F32) * weight_s[0, s]
             send_c[s] = rows.astype(BF16)
 
     send_all(send_c, recv_c, 1)
@@ -365,16 +376,16 @@
     def _(i):
         for j in range(4):
             t = i * 4 + j
-            first = recv_o[target_ref[2 * t]].astype(F32)
-            second = recv_o[target_ref[2 * t + 1]].astype(F32)
+            first = recv_o[index_s[1, t]].astype(F32)
+            second = recv_o[index_s[2, t]].astype(F32)
             grad = grd_t[t].astype(F32)
-            scr[row(t), :] = pair_weight_ref[2 * t] * first + pair_weight_ref[2 * t + 1] * second
+            scr[row(t), :] = weight_s[1, t] * first + weight_s[2, t] * second
             rg_a[pl.ds(t, 1), :] = jnp.sum(grad * first, axis=0, keepdims=True)
             rg_b[pl.ds(t, 1), :] = jnp.sum(grad * second, axis=0, keepdims=True)
 
     untiled(mixed_ref)
-    rg_ref[:, 0:1] = jnp.sum(rg_a[...], axis=1, keepdims=True)
-    rg_ref[:, 1:2] = jnp.sum(rg_b[...], axis=1, keepdims=True)
+    rg_ref[0:1, :] = jnp.sum(rg_a[...].T, axis=0, keepdims=True)
+    rg_ref[1:2, :] = jnp.sum(rg_b[...].T, axis=0, keepdims=True)
 
     wait_all(recv_r, a2a_recv.at[3])
 
@@ -382,8 +393,8 @@
     def _(i):
         for j in range(4):
             t = i * 4 + j
-            first = recv_r[target_ref[2 * t]].astype(F32)
-            second = recv_r[target_ref[2 * t + 1]].astype(F32)
+            first = recv_r[index_s[1, t]].astype(F32)
+            second = recv_r[index_s[2, t]].astype(F32)
             scr[row(t), :] = first + second
 
     untiled(gtok_ref)
@@ -400,20 +411,43 @@
                 near_copy(k, d, h).wait_send()
 
 
-def routing(expert_ids, route_weights, n_ep, cap):
-    assign = expert_ids.size
-    flat = expert_ids.reshape(-1)
-    order = jnp.arange(assign, dtype=jnp.int32)
-    earlier = (flat[:, None] == flat[None, :]) & (order[None, :] < order[:, None])
-    target = flat * cap + jnp.sum(earlier.astype(jnp.int32), axis=1)
-    slot = jnp.arange(n_ep * cap, dtype=jnp.int32)
-    match = slot[:, None] == target[None, :]
-    top = expert_ids.shape[1]
-    found = jnp.where(match, (order // top)[None, :] - expert_ids.shape[0], 0)
-    source = jnp.sum(found, axis=1) + expert_ids.shape[0]
-    weights = route_weights.reshape(-1).astype(F32)
-    slot_weight = jnp.sum(jnp.where(match, weights[None, :], 0.0), axis=1)
-    return source, slot_weight, target, weights
+def routing(ids_ref, pair_ref, index_v, weight_v, cap):
+    top, tok = ids_ref.shape
+    slots = index_v.shape[1]
+    here = lax.broadcasted_iota(jnp.int32, (tok, tok), 0)
+    there = lax.broadcasted_iota(jnp.int32, (tok, tok), 1)
+    rows = [jnp.broadcast_to(ids_ref[k : k + 1, :], (tok, tok)) for k in range(top)]
+    columns = [r.T for r in rows]
+    slot = lax.broadcasted_iota(jnp.int32, (tok, slots), 1)
+    token = lax.broadcasted_iota(jnp.int32, (tok, slots), 0)
+    source = jnp.full((1, slots), tok, jnp.int32)
+    weight = jnp.zeros((1, slots), F32)
+    for k in range(top):
+        rank = jnp.sum(
+            jnp.where((columns[k] == rows[k]) & (here < there), 1, 0), axis=0, keepdims=True
+        )
+        for m in range(k):
+            rank = rank + jnp.sum(jnp.where(columns[m] == rows[k], 1, 0), axis=0, keepdims=True)
+        target = ids_ref[k : k + 1, :] * cap + rank
+        pair = pair_ref[k : k + 1, :].astype(F32)
+        match = jnp.broadcast_to(target, (tok, tok)).T[:, 0:1] == slot
+        pairs = jnp.broadcast_to(pair, (tok, tok)).T[:, 0:1]
+        source = source + jnp.sum(jnp.where(match, token - tok, 0), axis=0, keepdims=True)
+        weight = weight + jnp.sum(jnp.where(match, pairs, 0.0), axis=0, keepdims=True)
+        index_v[1 + k : 2 + k, 0:tok] = target
+        weight_v[1 + k : 2 + k, 0:tok] = pair
+    index_v[0:1, :] = source
+    weight_v[0:1, :] = weight
+
+
+def copy_kernel(*refs):
+    n = (len(refs) - 1) // 2
+    sems = refs[-1]
+    copies = [pltpu.make_async_copy(refs[i], refs[n + i], sems.at[i]) for i in range(n)]
+    for copy in copies:
+        copy.start()
+    for copy in copies:
+        copy.wait()
 
 
 def per_device(n_rep, n_ep, tokens, expert_ids, route_weights, w_gate_up, w_down, grad_out):
@@ -425,23 +459,23 @@
     quarter = width // n_rep
     half = quarter // 2
     tiles = width // LANES
-    source, slot_weight, target, weights = routing(expert_ids, route_weights, n_ep, cap)
-    smem = pl.BlockSpec(memory_space=pltpu.SMEM)
+    padded = -(-slots // LANES) * LANES
     vmem = pl.BlockSpec(memory_space=pltpu.VMEM)
     anywhere = pl.BlockSpec(memory_space=pl.ANY)
     V = pltpu.VMEM
     rows = V((slots, tiles, LANES), BF16)
     dma = pltpu.SemaphoreType.DMA
-    mixed, gtok, ggu, gdn, rg = pl.pallas_call(
+    shapes = (
+        ((tok, width), BF16),
+        ((tok, width), BF16),
+        ((quarter, 2 * hidden), BF16),
+        ((quarter, hidden), BF16),
+        ((top, tok), F32),
+    )
+    made = pl.pallas_call(
         functools.partial(layer_kernel, (n_rep, n_ep, cap, tok, width, hidden)),
-        out_shape=(
-            jax.ShapeDtypeStruct((tok, width), BF16),
-            jax.ShapeDtypeStruct((tok, width), BF16),
-            jax.ShapeDtypeStruct((quarter, 2 * hidden), BF16),
-            jax.ShapeDtypeStruct((quarter, hidden), BF16),
-            jax.ShapeDtypeStruct((tok, top), F32),
-        ),
-        in_specs=[smem] * 4 + [vmem] * 2 + [anywhere] * 2,
+        out_shape=tuple(V(*shape) for shape in shapes),
+        in_specs=[vmem] * 4 + [anywhere] * 2,
         out_specs=[vmem] * 5,
         scratch_shapes=[
             V((n_rep, quarter, 2 * hidden), BF16),
@@ -468,7 +502,11 @@
             V((tok + 1, tiles, LANES), BF16),
             V((tok, LANES), F32),
             V((tok, LANES), F32),
-            dma((2,)),
+            V((8, padded), jnp.int32),
+            V((8, padded), F32),
+            pltpu.SMEM((8, padded), jnp.int32),
+            pltpu.SMEM((8, padded), F32),
+            dma((4,)),
             dma((2, 2, 2)),
             dma((2, 2, 2)),
             dma((2, 2)),
@@ -481,10 +519,18 @@
             dma((4,)),
         ],
         compiler_params=pltpu.CompilerParams(
-            collective_id=0, has_side_effects=True, vmem_limit_bytes=67043328
+            collective_id=0, has_side_effects=True, vmem_limit_bytes=62000000
         ),
-    )(source, slot_weight, target, weights, tokens, grad_out, w_gate_up[0], w_down[0])
-    return mixed, gtok, ggu[None], gdn[None], rg
+    )(expert_ids.T, route_weights.T, tokens, grad_out, w_gate_up[0], w_down[0])
+    mixed, gtok, ggu, gdn, rg = pl.pallas_call(
+        copy_kernel,
+        out_shape=tuple(jax.ShapeDtypeStruct(*shape) for shape in shapes),
+        in_specs=[vmem] * 5,
+        out_specs=[anywhere] * 5,
+        scratch_shapes=[dma((5,))],
+        compiler_params=pltpu.CompilerParams(vmem_limit_bytes=1 << 20),
+    )(*made)
+    return mixed, gtok, ggu[None], gdn[None], rg.T
 
 
 def solution(mesh):

time: 184 us -> 171 us (0.929)
  local copies, waits for them, and re-layouts: 10.3 us -> 0 us
    unnamed x14 -> x0, local copies, waits for them, and re-layouts: 9.26 us -> none
    pallas_call x1, Pallas kernels: 171 us -> 169 us  [per_device(): pl.pallas_call(functools.partial(layer_kernel, (n_rep, n_ep, cap, tok, wi...]
where the time goes in v2:
time: 171 us
  Pallas kernels  171 us (100%)
    pallas_call x1, Pallas kernels, per_device(): pl.pallas_call(functools.partial(layer_kernel, (n_rep, n_ep, cap, tok, wi...  169 us

profile of v2, /device:TPU:1, one launch (start us, length us, event | category | flops | bytes accessed | tf_op | source)
XLA Modules:
  0.0 171.2 jit_solution(6511769269108295536)
XLA Ops:
  0.6 168.7 %shard_map.101 = (bf16[128,2048]{1,0:T(8,128)(2,1)S(1)}, bf16[128,2048]{1,0:T(8,128)(2,1)S(1)}, bf16[512,1536]{1,0:T(8,128)(2,1)S(1)}, bf16[512,768]{1,0:T(8,128)(2,1)S(1)}, f32[2,128]{1,0:T(2,128)S(1)}) custom-call(s32[2,128]{1,0:T(2,128)} %bitcast.9, bf16[2,128]{1,0:T(2,128)(2,1)} %bitcast.10, bf16[128,2048]{1,0:T(8,128)(2,1)} %tokens_ref.1, ...), custom_call_target="tpu_custom_call" | custom-call | tf_op jit(solution)/shard_map/pallas_call | solution.py:475
  169.4 1.8 %shard_map.102 = (bf16[128,2048]{1,0:T(8,128)(2,1)}, bf16[128,2048]{1,0:T(8,128)(2,1)}, bf16[512,1536]{1,0:T(8,128)(2,1)}, bf16[512,768]{1,0:T(8,128)(2,1)}, f32[2,128]{1,0:T(2,128)}) custom-call(bf16[128,2048]{1,0:T(8,128)(2,1)S(1)} %get-tuple-element.15.refs_0_, bf16[128,2048]{1,0:T(8,128)(2,1)S(1)} %get-tuple-element.16.refs_1_, ...), custom_call_target="tpu_custom_call" | custom-call | tf_op jit(solution)/shard_map/pallas_call | solution.py:525

commit v3 on v2

v3 whole, which is shorter than its diff:
```python
import functools

import jax
import jax.numpy as jnp
from jax import lax
from jax.experimental import pallas as pl
from jax.experimental.pallas import tpu as pltpu
from jax.sharding import PartitionSpec as P

MESH = pl.DeviceIdType.MESH
F32 = jnp.float32
BF16 = jnp.bfloat16
LANES = 128


def layer_kernel(
    sizes,
    ids_ref,
    pair_ref,
    tokens_ref,
    grad_ref,
    wg_hbm,
    wd_hbm,
    mixed_ref,
    gtok_ref,
    ggu_ref,
    gdn_ref,
    rg_ref,
    wg,
    wd,
    part_g,
    part_d,
    pin_g,
    pin_d,
    home_g,
    home_d,
    relay_g,
    relay_d,
    back_g,
    back_d,
    din_g,
    din_d,
    send_x,
    recv_x,
    send_c,
    recv_c,
    send_o,
    recv_o,
    send_r,
    recv_r,
    x2,
    c2,
    scr,
    acc,
    gh,
    hid,
    ggu,
    tok_t,
    grd_t,
    rg_a,
    rg_b,
    index_v,
    weight_v,
    index_s,
    weight_s,
    local_sem,
    own_send,
    own_recv,
    out_send,
    out_recv,
    far_send,
    far_recv,
    fwd_send,
    fwd_recv,
    mate_send,
    mate_recv,
    swap_send,
    swap_recv,
    home_send,
    home_recv,
    near_send,
    near_recv,
    ret_send,
    ret_recv,
    fin_send,
    a2a_send,
    a2a_recv,
):
    n_rep, n_ep, cap, tok, width, hidden = sizes
    quarter = width // n_rep
    half = quarter // 2
    tiles = width // LANES
    per_q = quarter // LANES
    slots = n_ep * cap
    n_col = n_ep // 2
    x = lax.axis_index("rep")
    e = lax.axis_index("ep")
    col = e // 2
    core = lax.rem(e, 2)
    parity = lax.rem(x, 2)
    mate = 2 * col + 1 - core
    hosted = 2 * col + parity
    foreign = 2 * col + 1 - parity
    right = lax.rem(x + 1, n_rep)
    left = lax.rem(x + n_rep - 1, n_rep)
    ahead = lax.rem(x + 1 + 2 * core, n_rep)
    behind = lax.rem(x + 3 - 2 * core, n_rep)
    is_home = core == parity
    not_home = core != parity

    barrier = pltpu.get_barrier_semaphore()

    def greet(plane, index):
        pl.semaphore_signal(barrier, inc=1, device_id=(plane, index), device_id_type=MESH)

    greet(x, mate)
    greet(right, mate)
    greet(left, mate)
    greet(right, e)
    greet(left, e)

    @pl.loop(1, n_col)
    def _(i):
        other = 2 * lax.rem(col + i, n_col) + core
        greet(x, other)
        greet(right, other)
        greet(left, other)

    hbm = (wg_hbm, wd_hbm)
    full = (wg, wd)
    part = (part_g, part_d)
    pin = (pin_g, pin_d)
    home = (home_g, home_d)
    relay = (relay_g, relay_d)
    back = (back_g, back_d)
    din = (din_g, din_d)
    mine = pl.ds(pl.multiple_of(core * half, half), half)
    other_half = pl.ds(pl.multiple_of((1 - core) * half, half), half)
    halves = (pl.ds(0, half), pl.ds(half, half))
    sides = (right, left)

    def remote(src, dst, send, recv, plane, index):
        return pltpu.make_async_remote_copy(
            src_ref=src,
            dst_ref=dst,
            send_sem=send,
            recv_sem=recv,
            device_id=(plane, index),
            device_id_type=MESH,
        )

    def local_copy(k):
        return pltpu.make_async_copy(hbm[k], full[k].at[0], local_sem.at[k])

    def own_copy(k):
        return remote(hbm[k], full[k].at[0], own_send.at[k], own_recv.at[k], x, mate)

    def out_copy(k, d, h):
        return remote(
            hbm[k].at[halves[h], :],
            full[k].at[3 - 2 * d, halves[h], :],
            out_send.at[k, d, h],
            out_recv.at[k, d],
            sides[d],
            2 * col + h,
        )

    def far_copy(k, h):
        return remote(
            hbm[k].at[halves[h], :],
            relay[k],
            far_send.at[k, h],
            far_recv.at[k],
            sides[h],
            2 * col + h,
        )

    def fwd_copy(k):
        return remote(relay[k], full[k].at[2, mine, :], fwd_send.at[k], fwd_recv.at[k], ahead, e)

    def mate_copy(k, s):
        return remote(
            full[k].at[s, mine, :],
            full[k].at[s, mine, :],
            mate_send.at[k, s],
            mate_recv.at[k, s],
            x,
            mate,
        )

    def swap_copy(k, s):
        return remote(
            part[k].at[s, other_half, :],
            pin[k].at[s - 1],
            swap_send.at[k, s],
            swap_recv.at[k, s],
            x,
            mate,
        )

    def home_copy(k):
        return remote(part[k].at[0], home[k], home_send.at[k], home_recv.at[k], x, mate)

    def near_copy(k, d):
        return remote(
            part[k].at[1 + 2 * d, mine, :],
            din[k].at[d, mine, :],
            near_send.at[k, d],
            near_recv.at[k, d, core],
            sides[d],
            hosted,
        )

    def ret_copy(k):
        return remote(part[k].at[2, mine, :], back[k], ret_send.at[k], ret_recv.at[k], ahead, e)

    def fin_copy(k):
        return remote(
            back[k],
            din[k].at[0, mine, :],
            fin_send.at[k],
            near_recv.at[k, 0, core],
            ahead,
            foreign,
        )

    def send_rows(send, recv, n):
        def row_copy(plane, to, block, place):
            remote(
                send.at[pl.ds(block * cap, cap)],
                recv.at[pl.ds(place * cap, cap)],
                a2a_send.at[n],
                a2a_recv.at[n],
                plane,
                2 * to + core,
            ).start()

        row_copy(ahead, col, foreign, n_col + col)

        @pl.loop(1, n_col)
        def _(i):
            to = lax.rem(col + i, n_col)
            row_copy(x, to, 2 * to + parity, col)
            row_copy(ahead, to, 2 * to + 1 - parity, n_col + col)

        recv[pl.ds(col * cap, cap)] = send[pl.ds(hosted * cap, cap)]

    def return_rows(send, recv, n):
        def row_copy(plane, to, block):
            remote(
                send.at[pl.ds(block * cap, cap)],
                recv.at[pl.ds(hosted * cap, cap)],
                a2a_send.at[n],
                a2a_recv.at[n],
                plane,
                2 * to + core,
            ).start()

        row_copy(behind, col, n_col + col)

        @pl.loop(1, n_col)
        def _(i):
            to = lax.rem(col + i, n_col)
            row_copy(x, to, to)
            row_copy(behind, to, n_col + to)

        recv[pl.ds(hosted * cap, cap)] = send[pl.ds(col * cap, cap)]

    def wait_all(buf, sem):
        rest = buf.at[pl.ds(0, (n_ep - 1) * cap)]
        pltpu.make_async_copy(rest, rest, sem).wait()

    def tiled(src, dst):
        for j in range(tiles):
            scr[pl.ds(j, tok, stride=tiles), :] = src[:, j * LANES : (j + 1) * LANES].astype(F32)

        @pl.loop(0, tok // 8)
        def _(i):
            rows = pl.ds(pl.multiple_of(i * 8 * tiles, 16), 8 * tiles)
            dst[pl.ds(i * 8, 8)] = scr[rows, :].astype(BF16).reshape(8, tiles, LANES)

        dst[tok] = jnp.zeros((tiles, LANES), BF16)

    def row(r):
        return pl.ds(pl.multiple_of(r * tiles, 16), tiles)

    @pl.when(is_home)
    def _():
        for k in range(2):
            local_copy(k).start()

    tables = [
        pltpu.make_async_copy(index_v, index_s, local_sem.at[2]),
        pltpu.make_async_copy(weight_v, weight_s, local_sem.at[3]),
    ]
    routing(ids_ref, pair_ref, index_v, weight_v, cap)
    for copy in tables:
        copy.start()
    tiled(tokens_ref, tok_t)
    for copy in tables:
        copy.wait()

    @pl.loop(0, slots // 8)
    def _(i):
        for j in range(8):
            s = i * 8 + j
            send_x[s] = tok_t[index_s[0, s]]

    pl.semaphore_wait(barrier, 3 * n_col + 2)

    @pl.when(is_home)
    def _():
        for k in range(2):
            for h in range(2):
                far_copy(k, h).start()
        for k in range(2):
            own_copy(k).start()

    @pl.when(not_home)
    def _():
        for k in range(2):
            for h in range(2):
                for d in range(2):
                    out_copy(k, d, h).start()

    send_rows(send_x, recv_x, 0)
    tiled(grad_ref, grd_t)

    @pl.loop(0, slots // 8)
    def _(i):
        for j in range(8):
            s = i * 8 + j
            rows = grd_t[index_s[0, s]].astype(F32) * weight_s[0, s]
            send_c[s] = rows.astype(BF16)

    send_rows(send_c, recv_c, 1)

    def spread(recv, dst):
        @pl.loop(0, slots // 8)
        def _(i):
            rows = pl.ds(pl.multiple_of(i * 8 * tiles, 16), 8 * tiles)
            scr[rows, :] = recv[pl.ds(i * 8, 8)].astype(F32).reshape(8 * tiles, LANES)

        for q in range(n_rep):
            for j in range(per_q):
                dst[q, :, j * LANES : (j + 1) * LANES] = scr[
                    pl.ds(q * per_q + j, slots, stride=tiles), :
                ].astype(BF16)

    def place(s):
        return lax.rem(x + s, n_rep)

    def product(s, lhs, rhs, out, columns, step, first):
        @pl.loop(0, columns // step)
        def _(n):
            cols = pl.ds(pl.multiple_of(n * step, LANES), step)
            y = jnp.dot(lhs[place(s)], rhs[s, :, cols], preferred_element_type=F32)
            if first:
                out[:, cols] = y
            else:
                out[:, cols] = out[:, cols] + y

    def returned(lhs, rhs, send):
        for q in range(n_rep):
            s = lax.rem(q + n_rep - x, n_rep)
            for j in range(per_q):
                scr[pl.ds(q * per_q + j, slots, stride=tiles), :] = lax.dot_general(
                    lhs[...],
                    rhs[s, j * LANES : (j + 1) * LANES, :],
                    (((1,), (1,)), ((), ())),
                    preferred_element_type=F32,
                )

        @pl.loop(0, slots // 8)
        def _(i):
            rows = pl.ds(pl.multiple_of(i * 8 * tiles, 16), 8 * tiles)
            send[pl.ds(i * 8, 8)] = scr[rows, :].astype(BF16).reshape(8, tiles, LANES)

    def outer(lhs, rhs, s, rows, k, columns, step):
        block = lhs[place(s), :, rows]

        @pl.loop(0, columns // step)
        def _(n):
            cols = pl.ds(pl.multiple_of(n * step, LANES), step)
            y = lax.dot_general(
                block, rhs[:, cols], (((0,), (0,)), ((), ())), preferred_element_type=F32
            )
            part[k][s, rows, cols] = y.astype(BF16)

    def partial_grads(lhs, rhs, k, columns, step):
        for s in (2, 1, 3):
            outer(lhs, rhs, s, other_half, k, columns, step)
            swap_copy(k, s).start()
        for s in (2, 1, 3):
            outer(lhs, rhs, s, mine, k, columns, step)
            swap_copy(k, s).wait_recv()

            @pl.loop(0, half // 16)
            def _(i):
                here = pl.ds(pl.multiple_of(i * 16, 16), 16)
                there = pl.ds(pl.multiple_of(core * half + i * 16, 16), 16)
                total = part[k][s, there, :].astype(F32) + pin[k][s - 1, here, :].astype(F32)
                part[k][s, there, :] = total.astype(BF16)

            if s == 2:
                ret_copy(k).start()
            else:
                near_copy(k, s // 2).start()
        for h in range(2):
            outer(lhs, rhs, 0, halves[h], k, columns, step)

        @pl.when(not_home)
        def _():
            home_copy(k).start()

    def pass_on(k):
        ret_copy(k).wait_recv()
        fin_copy(k).start()

    def finish(k, out):
        @pl.when(is_home)
        def _():
            home_copy(k).wait_recv()

        for h in range(2):
            arrived = [
                remote(
                    back[k], din[k].at[d, halves[h], :], fin_send.at[k], near_recv.at[k, d, h], x, mate
                )
                for d in range(2)
            ]
            arrived[0].wait_recv()

            @pl.when(is_home)
            def _():
                @pl.loop(0, half // 16)
                def _(i):
                    rows = pl.ds(pl.multiple_of(h * half + i * 16, 16), 16)
                    total = part[k][0, rows, :].astype(F32) + home[k][rows, :].astype(F32)
                    out[rows, :] = (total + din[k][0, rows, :].astype(F32)).astype(BF16)

            @pl.when(not_home)
            def _():
                arrived[1].wait_recv()

                @pl.loop(0, half // 16)
                def _(i):
                    rows = pl.ds(pl.multiple_of(h * half + i * 16, 16), 16)
                    total = din[k][0, rows, :].astype(F32) + din[k][1, rows, :].astype(F32)
                    out[rows, :] = total.astype(BF16)

    def near_arrives(k):
        for d in range(2):
            out_copy(k, d, 0).wait_recv()
            mate_copy(k, 3 - 2 * d).start()

    def far_arrives(k):
        fwd_copy(k).wait_recv()
        mate_copy(k, 2).start()

    def own_arrives(k):
        @pl.when(is_home)
        def _():
            local_copy(k).wait()

        @pl.when(not_home)
        def _():
            own_copy(k).wait_recv()

    for k in range(2):
        far_copy(k, 0).wait_recv()
        fwd_copy(k).start()
    wait_all(recv_x, a2a_recv.at[0])
    spread(recv_x, x2)
    own_arrives(0)
    product(0, x2, wg, acc, 2 * hidden, 256, True)
    near_arrives(0)
    for s in (1, 3):
        mate_copy(0, s).wait_recv()
        product(s, x2, wg, acc, 2 * hidden, 256, False)
    near_arrives(1)
    far_arrives(0)
    mate_copy(0, 2).wait_recv()
    product(2, x2, wg, acc, 2 * hidden, 256, False)

    @pl.loop(0, slots // 16)
    def _(i):
        rows = pl.ds(pl.multiple_of(i * 16, 16), 16)
        gate = acc[rows, :hidden]
        up = acc[rows, hidden:]
        hid[rows, :] = (gate * jax.nn.sigmoid(gate) * up).astype(BF16)

    far_arrives(1)
    own_arrives(1)
    for s in (1, 3, 2):
        mate_copy(1, s).wait_recv()
    returned(hid, wd, send_o)
    return_rows(send_o, recv_o, 2)

    wait_all(recv_c, a2a_recv.at[1])
    spread(recv_c, c2)
    partial_grads(c2, hid, 1, hidden, 256)
    for s in range(n_rep):
        product(s, c2, wd, gh, hidden, 256, s == 0)

    @pl.loop(0, slots // 16)
    def _(i):
        rows = pl.ds(pl.multiple_of(i * 16, 16), 16)
        gate = acc[rows, :hidden]
        up = acc[rows, hidden:]
        grad = gh[rows, :]
        s = jax.nn.sigmoid(gate)
        ggu[rows, :hidden] = (grad * up * (s * (1.0 + gate * (1.0 - s)))).astype(BF16)
        ggu[rows, hidden:] = (grad * gate * s).astype(BF16)

    returned(ggu, wg, send_r)
    return_rows(send_r, recv_r, 3)
    pass_on(1)
    partial_grads(x2, ggu, 0, 2 * hidden, 256)

    def untiled(out):
        for j in range(tiles):
            out[:, j * LANES : (j + 1) * LANES] = scr[pl.ds(j, tok, stride=tiles), :].astype(BF16)

    wait_all(recv_o, a2a_recv.at[2])

    @pl.loop(0, tok // 4)
    def _(i):
        for j in range(4):
            t = i * 4 + j
            first = recv_o[index_s[1, t]].astype(F32)
            second = recv_o[index_s[2, t]].astype(F32)
            grad = grd_t[t].astype(F32)
            scr[row(t), :] = weight_s[1, t] * first + weight_s[2, t] * second
            rg_a[pl.ds(t, 1), :] = jnp.sum(grad * first, axis=0, keepdims=True)
            rg_b[pl.ds(t, 1), :] = jnp.sum(grad * second, axis=0, keepdims=True)

    untiled(mixed_ref)
    rg_ref[0:1, :] = jnp.sum(rg_a[...].T, axis=0, keepdims=True)
    rg_ref[1:2, :] = jnp.sum(rg_b[...].T, axis=0, keepdims=True)

    pass_on(0)
    finish(1, gdn_ref)
    wait_all(recv_r, a2a_recv.at[3])

    @pl.loop(0, tok // 4)
    def _(i):
        for j in range(4):
            t = i * 4 + j
            first = recv_r[index_s[1, t]].astype(F32)
            second = recv_r[index_s[2, t]].astype(F32)
            scr[row(t), :] = first + second

    untiled(gtok_ref)
    finish(0, ggu_ref)

    for n, buf in enumerate((send_x, send_c, send_o, send_r)):
        wait_all(buf, a2a_send.at[n])
    for k in range(2):
        fwd_copy(k).wait_send()
        ret_copy(k).wait_send()
        fin_copy(k).wait_send()
        for s in (1, 2, 3):
            mate_copy(k, s).wait_send()
            swap_copy(k, s).wait_send()
        for d in range(2):
            near_copy(k, d).wait_send()

    @pl.when(is_home)
    def _():
        for k in range(2):
            own_copy(k).wait_send()
            for h in range(2):
                far_copy(k, h).wait_send()

    @pl.when(not_home)
    def _():
        for k in range(2):
            home_copy(k).wait_send()
            for d in range(2):
                for h in range(2):
                    out_copy(k, d, h).wait_send()


def routing(ids_ref, pair_ref, index_v, weight_v, cap):
    top, tok = ids_ref.shape
    slots = index_v.shape[1]
    here = lax.broadcasted_iota(jnp.int32, (tok, tok), 0)
    there = lax.broadcasted_iota(jnp.int32, (tok, tok), 1)
    rows = [jnp.broadcast_to(ids_ref[k : k + 1, :], (tok, tok)) for k in range(top)]
    columns = [r.T for r in rows]
    slot = lax.broadcasted_iota(jnp.int32, (tok, slots), 1)
    token = lax.broadcasted_iota(jnp.int32, (tok, slots), 0)
    source = jnp.full((1, slots), tok, jnp.int32)
    weight = jnp.zeros((1, slots), F32)
    for k in range(top):
        rank = jnp.sum(
            jnp.where((columns[k] == rows[k]) & (here < there), 1, 0), axis=0, keepdims=True
        )
        for m in range(k):
            rank = rank + jnp.sum(jnp.where(columns[m] == rows[k], 1, 0), axis=0, keepdims=True)
        target = ids_ref[k : k + 1, :] * cap + rank
        pair = pair_ref[k : k + 1, :].astype(F32)
        match = jnp.broadcast_to(target, (tok, tok)).T[:, 0:1] == slot
        pairs = jnp.broadcast_to(pair, (tok, tok)).T[:, 0:1]
        source = source + jnp.sum(jnp.where(match, token - tok, 0), axis=0, keepdims=True)
        weight = weight + jnp.sum(jnp.where(match, pairs, 0.0), axis=0, keepdims=True)
        index_v[1 + k : 2 + k, 0:tok] = target
        weight_v[1 + k : 2 + k, 0:tok] = pair
    index_v[0:1, :] = source
    weight_v[0:1, :] = weight


def copy_kernel(*refs):
    n = (len(refs) - 1) // 2
    sems = refs[-1]
    copies = [pltpu.make_async_copy(refs[i], refs[n + i], sems.at[i]) for i in range(n)]
    for copy in copies:
        copy.start()
    for copy in copies:
        copy.wait()


def per_device(n_rep, n_ep, tokens, expert_ids, route_weights, w_gate_up, w_down, grad_out):
    tok, width = tokens.shape
    top = expert_ids.shape[1]
    hidden = w_down.shape[2]
    cap = 5 * tok * top // (4 * n_ep)
    slots = n_ep * cap
    quarter = width // n_rep
    half = quarter // 2
    tiles = width // LANES
    padded = -(-slots // LANES) * LANES
    vmem = pl.BlockSpec(memory_space=pltpu.VMEM)
    anywhere = pl.BlockSpec(memory_space=pl.ANY)
    V = pltpu.VMEM
    rows = V((slots, tiles, LANES), BF16)
    dma = pltpu.SemaphoreType.DMA
    shapes = (
        ((tok, width), BF16),
        ((tok, width), BF16),
        ((quarter, 2 * hidden), BF16),
        ((quarter, hidden), BF16),
        ((top, tok), F32),
    )
    made = pl.pallas_call(
        functools.partial(layer_kernel, (n_rep, n_ep, cap, tok, width, hidden)),
        out_shape=tuple(V(*shape) for shape in shapes),
        in_specs=[vmem] * 4 + [anywhere] * 2,
        out_specs=[vmem] * 5,
        scratch_shapes=[
            V(lead + (rows_, width_), BF16)
            for lead, rows_ in (
                ((n_rep,), quarter),
                ((n_rep,), quarter),
                ((n_rep - 1,), half),
                ((), quarter),
                ((), half),
                ((), half),
                ((2,), quarter),
            )
            for width_ in (2 * hidden, hidden)
        ]
        + [rows] * 8
        + [
            V((n_rep, slots, quarter), BF16),
            V((n_rep, slots, quarter), BF16),
            V((slots * tiles, LANES), F32),
            V((slots, 2 * hidden), F32),
            V((slots, hidden), F32),
            V((slots, hidden), BF16),
            V((slots, 2 * hidden), BF16),
            V((tok + 1, tiles, LANES), BF16),
            V((tok + 1, tiles, LANES), BF16),
            V((tok, LANES), F32),
            V((tok, LANES), F32),
            V((8, padded), jnp.int32),
            V((8, padded), F32),
            pltpu.SMEM((8, padded), jnp.int32),
            pltpu.SMEM((8, padded), F32),
            dma((4,)),
            dma((2,)),
            dma((2,)),
            dma((2, 2, 2)),
            dma((2, 2)),
            dma((2, 2)),
            dma((2,)),
            dma((2,)),
            dma((2,)),
            dma((2, n_rep)),
            dma((2, n_rep)),
            dma((2, n_rep)),
            dma((2, n_rep)),
            dma((2,)),
            dma((2,)),
            dma((2, 2)),
            dma((2, 2, 2)),
            dma((2,)),
            dma((2,)),
            dma((2,)),
            dma((4,)),
            dma((4,)),
        ],
        compiler_params=pltpu.CompilerParams(
            collective_id=0, has_side_effects=True, vmem_limit_bytes=62000000
        ),
    )(expert_ids.T, route_weights.T, tokens, grad_out, w_gate_up[0], w_down[0])
    mixed, gtok, ggu, gdn, rg = pl.pallas_call(
        copy_kernel,
        out_shape=tuple(jax.ShapeDtypeStruct(*shape) for shape in shapes),
        in_specs=[vmem] * 5,
        out_specs=[anywhere] * 5,
        scratch_shapes=[dma((5,))],
        compiler_params=pltpu.CompilerParams(vmem_limit_bytes=1 << 20),
    )(*made)
    return mixed, gtok, ggu[None], gdn[None], rg.T


def solution(mesh):
    both = ("rep", "ep")
    split = P(both, None)
    weights = P("ep", "rep", None)
    return jax.shard_map(
        functools.partial(per_device, mesh.shape["rep"], mesh.shape["ep"]),
        mesh=mesh,
        in_specs=(split, split, split, weights, weights, split),
        out_specs=(split, split, weights, weights, split),
        check_vma=False,
    )
```

time: 171 us -> 161 us (0.942); the launches traced: 171 us -> 159 us
  Pallas kernels: 171 us -> 159 us
    pallas_call x1, Pallas kernels: 169 us -> 157 us  [per_device(): pl.pallas_call(functools.partial(layer_kernel, (n_rep, n_ep, cap, tok, wi...]
where the time goes in v3:
time: 161 us; the launch traced here: 159 us
  Pallas kernels  159 us (99%)
    pallas_call x1, Pallas kernels, per_device(): pl.pallas_call(functools.partial(layer_kernel, (n_rep, n_ep, cap, tok, wi...  157 us

profile of v3, /device:TPU:1, one launch (start us, length us, event | category | flops | bytes accessed | tf_op | source)
XLA Modules:
  0.0 159.4 jit_solution(7749672624808703966)
XLA Ops:
  0.6 156.9 %shard_map.101 = (bf16[128,2048]{1,0:T(8,128)(2,1)S(1)}, bf16[128,2048]{1,0:T(8,128)(2,1)S(1)}, bf16[512,1536]{1,0:T(8,128)(2,1)S(1)}, bf16[512,768]{1,0:T(8,128)(2,1)S(1)}, f32[2,128]{1,0:T(2,128)S(1)}) custom-call(s32[2,128]{1,0:T(2,128)} %bitcast.9, bf16[2,128]{1,0:T(2,128)(2,1)} %bitcast.10, bf16[128,2048]{1,0:T(8,128)(2,1)} %tokens_ref.1, ...), custom_call_target="tpu_custom_call" | custom-call | tf_op jit(solution)/shard_map/pallas_call | solution.py:646
  157.6 1.8 %shard_map.102 = (bf16[128,2048]{1,0:T(8,128)(2,1)}, bf16[128,2048]{1,0:T(8,128)(2,1)}, bf16[512,1536]{1,0:T(8,128)(2,1)}, bf16[512,768]{1,0:T(8,128)(2,1)}, f32[2,128]{1,0:T(2,128)}) custom-call(bf16[128,2048]{1,0:T(8,128)(2,1)S(1)} %get-tuple-element.15.refs_0_, bf16[128,2048]{1,0:T(8,128)(2,1)S(1)} %get-tuple-element.16.refs_1_, ...), custom_call_target="tpu_custom_call" | custom-call | tf_op jit(solution)/shard_map/pallas_call | solution.py:708

commit v4 on v3

--- a/solution.py
+++ b/solution.py
@@ -85,6 +85,7 @@
     fin_send,
     a2a_send,
     a2a_recv,
+    ready,
 ):
     n_rep, n_ep, cap, tok, width, hidden = sizes
     quarter = width // n_rep
@@ -113,18 +114,34 @@
     def greet(plane, index):
         pl.semaphore_signal(barrier, inc=1, device_id=(plane, index), device_id_type=MESH)
 
+    ny, nz = 4, n_col // 4
+    yy, zz = col // nz, lax.rem(col, nz)
+
+    def beside(dy, dz):
+        return (lax.rem(yy + dy, ny) * nz + lax.rem(zz + dz, nz)) * 2 + core
+
+    near = [beside(1, 0), beside(ny - 1, 0), beside(0, 1), beside(0, nz - 1)]
     greet(x, mate)
-    greet(right, mate)
-    greet(left, mate)
-    greet(right, e)
-    greet(left, e)
-
-    @pl.loop(1, n_col)
-    def _(i):
-        other = 2 * lax.rem(col + i, n_col) + core
-        greet(x, other)
-        greet(right, other)
-        greet(left, other)
+    for plane in (right, left):
+        greet(plane, mate)
+        greet(plane, e)
+    for index in near:
+        greet(x, index)
+    rounds = (
+        [(x, index) for index in near],
+        [(x, beside(0, 2)), (x, beside(0, nz - 2))],
+        [(x, beside(dy, 0)) for dy in range(1, ny)],
+        [(right, e), (left, e)],
+    )
+
+    def tell(r):
+        for plane, index in rounds[r]:
+            pl.semaphore_signal(
+                ready.at[r], inc=1, device_id=(plane, index), device_id_type=MESH
+            )
+
+    def hear(r):
+        pl.semaphore_wait(ready.at[r], len(rounds[r]))
 
     hbm = (wg_hbm, wd_hbm)
     full = (wg, wd)
@@ -289,6 +306,24 @@
         for k in range(2):
             local_copy(k).start()
 
+    pl.semaphore_wait(barrier, 9)
+
+    @pl.when(is_home)
+    def _():
+        for k in range(2):
+            for h in range(2):
+                far_copy(k, h).start()
+        for k in range(2):
+            own_copy(k).start()
+
+    @pl.when(not_home)
+    def _():
+        for k in range(2):
+            for h in range(2):
+                for d in range(2):
+                    out_copy(k, d, h).start()
+
+    tell(0)
     tables = [
         pltpu.make_async_copy(index_v, index_s, local_sem.at[2]),
         pltpu.make_async_copy(weight_v, weight_s, local_sem.at[3]),
@@ -296,7 +331,11 @@
     routing(ids_ref, pair_ref, index_v, weight_v, cap)
     for copy in tables:
         copy.start()
+    hear(0)
+    tell(1)
     tiled(tokens_ref, tok_t)
+    hear(1)
+    tell(2)
     for copy in tables:
         copy.wait()
 
@@ -306,25 +345,11 @@
             s = i * 8 + j
             send_x[s] = tok_t[index_s[0, s]]
 
-    pl.semaphore_wait(barrier, 3 * n_col + 2)
-
-    @pl.when(is_home)
-    def _():
-        for k in range(2):
-            for h in range(2):
-                far_copy(k, h).start()
-        for k in range(2):
-            own_copy(k).start()
-
-    @pl.when(not_home)
-    def _():
-        for k in range(2):
-            for h in range(2):
-                for d in range(2):
-                    out_copy(k, d, h).start()
-
+    hear(2)
+    tell(3)
+    tiled(grad_ref, grd_t)
+    hear(3)
     send_rows(send_x, recv_x, 0)
-    tiled(grad_ref, grd_t)
 
     @pl.loop(0, slots // 8)
     def _(i):
@@ -473,15 +498,15 @@
     wait_all(recv_x, a2a_recv.at[0])
     spread(recv_x, x2)
     own_arrives(0)
-    product(0, x2, wg, acc, 2 * hidden, 256, True)
+    product(0, x2, wg, acc, 2 * hidden, 768, True)
     near_arrives(0)
     for s in (1, 3):
         mate_copy(0, s).wait_recv()
-        product(s, x2, wg, acc, 2 * hidden, 256, False)
+        product(s, x2, wg, acc, 2 * hidden, 768, False)
     near_arrives(1)
     far_arrives(0)
     mate_copy(0, 2).wait_recv()
-    product(2, x2, wg, acc, 2 * hidden, 256, False)
+    product(2, x2, wg, acc, 2 * hidden, 768, False)
 
     @pl.loop(0, slots // 16)
     def _(i):
@@ -499,9 +524,9 @@
 
     wait_all(recv_c, a2a_recv.at[1])
     spread(recv_c, c2)
-    partial_grads(c2, hid, 1, hidden, 256)
+    partial_grads(c2, hid, 1, hidden, 768)
     for s in range(n_rep):
-        product(s, c2, wd, gh, hidden, 256, s == 0)
+        product(s, c2, wd, gh, hidden, 768, s == 0)
 
     @pl.loop(0, slots // 16)
     def _(i):
@@ -516,7 +541,7 @@
     returned(ggu, wg, send_r)
     return_rows(send_r, recv_r, 3)
     pass_on(1)
-    partial_grads(x2, ggu, 0, 2 * hidden, 256)
+    partial_grads(x2, ggu, 0, 2 * hidden, 768)
 
     def untiled(out):
         for j in range(tiles):
@@ -700,6 +725,7 @@
             dma((2,)),
             dma((4,)),
             dma((4,)),
+            pltpu.SemaphoreType.REGULAR((4,)),
         ],
         compiler_params=pltpu.CompilerParams(
             collective_id=0, has_side_effects=True, vmem_limit_bytes=62000000

time: 161 us -> 155 us (0.963)
  Pallas kernels: 159 us -> 152 us
    pallas_call x1, Pallas kernels: 157 us -> 151 us  [per_device(): pl.pallas_call(functools.partial(layer_kernel, (n_rep, n_ep, cap, tok, wi...]
where the time goes in v4:
time: 155 us; the launch traced here: 153 us
  Pallas kernels  152 us (98%)
    pallas_call x1, Pallas kernels, per_device(): pl.pallas_call(functools.partial(layer_kernel, (n_rep, n_ep, cap, tok, wi...  151 us

profile of v4, /device:TPU:1, one launch (start us, length us, event | category | flops | bytes accessed | tf_op | source)
XLA Modules:
  0.0 153.2 jit_solution(14246605353013986889)
XLA Ops:
  0.6 150.6 %shard_map.101 = (bf16[128,2048]{1,0:T(8,128)(2,1)S(1)}, bf16[128,2048]{1,0:T(8,128)(2,1)S(1)}, bf16[512,1536]{1,0:T(8,128)(2,1)S(1)}, bf16[512,768]{1,0:T(8,128)(2,1)S(1)}, f32[2,128]{1,0:T(2,128)S(1)}) custom-call(s32[2,128]{1,0:T(2,128)} %bitcast.9, bf16[2,128]{1,0:T(2,128)(2,1)} %bitcast.10, bf16[128,2048]{1,0:T(8,128)(2,1)} %tokens_ref.1, ...), custom_call_target="tpu_custom_call" | custom-call | tf_op jit(solution)/shard_map/pallas_call | solution.py:671
  151.3 1.8 %shard_map.102 = (bf16[128,2048]{1,0:T(8,128)(2,1)}, bf16[128,2048]{1,0:T(8,128)(2,1)}, bf16[512,1536]{1,0:T(8,128)(2,1)}, bf16[512,768]{1,0:T(8,128)(2,1)}, f32[2,128]{1,0:T(2,128)}) custom-call(bf16[128,2048]{1,0:T(8,128)(2,1)S(1)} %get-tuple-element.15.refs_0_, bf16[128,2048]{1,0:T(8,128)(2,1)S(1)} %get-tuple-element.16.refs_1_, ...), custom_call_target="tpu_custom_call" | custom-call | tf_op jit(solution)/shard_map/pallas_call | solution.py:734

commit v5 on v4

--- a/solution.py
+++ b/solution.py
@@ -416,6 +416,8 @@
         for s in (2, 1, 3):
             outer(lhs, rhs, s, other_half, k, columns, step)
             swap_copy(k, s).start()
+        if k == 1:
+            far_arrives(1)
         for s in (2, 1, 3):
             outer(lhs, rhs, s, mine, k, columns, step)
             swap_copy(k, s).wait_recv()
@@ -431,6 +433,8 @@
                 ret_copy(k).start()
             else:
                 near_copy(k, s // 2).start()
+
+    def home_grads(lhs, rhs, k, columns, step):
         for h in range(2):
             outer(lhs, rhs, 0, halves[h], k, columns, step)
 
@@ -515,16 +519,14 @@
         up = acc[rows, hidden:]
         hid[rows, :] = (gate * jax.nn.sigmoid(gate) * up).astype(BF16)
 
-    far_arrives(1)
+    wait_all(recv_c, a2a_recv.at[1])
+    spread(recv_c, c2)
+    partial_grads(c2, hid, 1, hidden, 768)
     own_arrives(1)
     for s in (1, 3, 2):
         mate_copy(1, s).wait_recv()
     returned(hid, wd, send_o)
     return_rows(send_o, recv_o, 2)
-
-    wait_all(recv_c, a2a_recv.at[1])
-    spread(recv_c, c2)
-    partial_grads(c2, hid, 1, hidden, 768)
     for s in range(n_rep):
         product(s, c2, wd, gh, hidden, 768, s == 0)
 
@@ -542,6 +544,8 @@
     return_rows(send_r, recv_r, 3)
     pass_on(1)
     partial_grads(x2, ggu, 0, 2 * hidden, 768)
+    home_grads(c2, hid, 1, hidden, 768)
+    home_grads(x2, ggu, 0, 2 * hidden, 768)
 
     def untiled(out):
         for j in range(tiles):

time: 155 us -> 153 us (0.987)
  Pallas kernels: 152 us -> 150 us
    pallas_call x1, Pallas kernels: 151 us -> 148 us  [per_device(): pl.pallas_call(functools.partial(layer_kernel, (n_rep, n_ep, cap, tok, wi...]
where the time goes in v5:
time: 153 us; the launch traced here: 150 us
  Pallas kernels  150 us (98%)
    pallas_call x1, Pallas kernels, per_device(): pl.pallas_call(functools.partial(layer_kernel, (n_rep, n_ep, cap, tok, wi...  148 us

profile of v5, /device:TPU:1, one launch (start us, length us, event | category | flops | bytes accessed | tf_op | source)
XLA Modules:
  0.0 150.5 jit_solution(2122423974508813850)
XLA Ops:
  0.6 147.9 %shard_map.101 = (bf16[128,2048]{1,0:T(8,128)(2,1)S(1)}, bf16[128,2048]{1,0:T(8,128)(2,1)S(1)}, bf16[512,1536]{1,0:T(8,128)(2,1)S(1)}, bf16[512,768]{1,0:T(8,128)(2,1)S(1)}, f32[2,128]{1,0:T(2,128)S(1)}) custom-call(s32[2,128]{1,0:T(2,128)} %bitcast.9, bf16[2,128]{1,0:T(2,128)(2,1)} %bitcast.10, bf16[128,2048]{1,0:T(8,128)(2,1)} %tokens_ref.1, ...), custom_call_target="tpu_custom_call" | custom-call | tf_op jit(solution)/shard_map/pallas_call | solution.py:675
  148.5 1.8 %shard_map.102 = (bf16[128,2048]{1,0:T(8,128)(2,1)}, bf16[128,2048]{1,0:T(8,128)(2,1)}, bf16[512,1536]{1,0:T(8,128)(2,1)}, bf16[512,768]{1,0:T(8,128)(2,1)}, f32[2,128]{1,0:T(2,128)}) custom-call(bf16[128,2048]{1,0:T(8,128)(2,1)S(1)} %get-tuple-element.15.refs_0_, bf16[128,2048]{1,0:T(8,128)(2,1)S(1)} %get-tuple-element.16.refs_1_, ...), custom_call_target="tpu_custom_call" | custom-call | tf_op jit(solution)/shard_map/pallas_call | solution.py:738

commit v6 on v5

--- a/solution.py
+++ b/solution.py
@@ -540,10 +540,10 @@
         ggu[rows, :hidden] = (grad * up * (s * (1.0 + gate * (1.0 - s)))).astype(BF16)
         ggu[rows, hidden:] = (grad * gate * s).astype(BF16)
 
+    pass_on(1)
+    partial_grads(x2, ggu, 0, 2 * hidden, 768)
     returned(ggu, wg, send_r)
     return_rows(send_r, recv_r, 3)
-    pass_on(1)
-    partial_grads(x2, ggu, 0, 2 * hidden, 768)
     home_grads(c2, hid, 1, hidden, 768)
     home_grads(x2, ggu, 0, 2 * hidden, 768)
 

time: 153 us -> 153 us (level)
  no operation moved by 1% of the time
where the time goes in v6:
time: 153 us; the launch traced here: 150 us
  Pallas kernels  150 us (98%)
    pallas_call x1, Pallas kernels, per_device(): pl.pallas_call(functools.partial(layer_kernel, (n_rep, n_ep, cap, tok, wi...  148 us

profile of v6, /device:TPU:1, one launch (start us, length us, event | category | flops | bytes accessed | tf_op | source)
XLA Modules:
  0.0 150.5 jit_solution(17934091025774208353)
XLA Ops:
  0.6 147.9 %shard_map.101 = (bf16[128,2048]{1,0:T(8,128)(2,1)S(1)}, bf16[128,2048]{1,0:T(8,128)(2,1)S(1)}, bf16[512,1536]{1,0:T(8,128)(2,1)S(1)}, bf16[512,768]{1,0:T(8,128)(2,1)S(1)}, f32[2,128]{1,0:T(2,128)S(1)}) custom-call(s32[2,128]{1,0:T(2,128)} %bitcast.9, bf16[2,128]{1,0:T(2,128)(2,1)} %bitcast.10, bf16[128,2048]{1,0:T(8,128)(2,1)} %tokens_ref.1, ...), custom_call_target="tpu_custom_call" | custom-call | tf_op jit(solution)/shard_map/pallas_call | solution.py:675
  148.5 1.8 %shard_map.102 = (bf16[128,2048]{1,0:T(8,128)(2,1)}, bf16[128,2048]{1,0:T(8,128)(2,1)}, bf16[512,1536]{1,0:T(8,128)(2,1)}, bf16[512,768]{1,0:T(8,128)(2,1)}, f32[2,128]{1,0:T(2,128)}) custom-call(bf16[128,2048]{1,0:T(8,128)(2,1)S(1)} %get-tuple-element.15.refs_0_, bf16[128,2048]{1,0:T(8,128)(2,1)S(1)} %get-tuple-element.16.refs_1_, ...), custom_call_target="tpu_custom_call" | custom-call | tf_op jit(solution)/shard_map/pallas_call | solution.py:738
